TPU v7x, 512 devices: a whole 4x4x16 slice. The times are simulated.
512 devices in a mesh: gz: 128 (over z, y, core), gy: 4 (over x).
Axes of the slice: x: 4, y: 4, z: 16, core: 2. Of those that a mesh axis runs over, the one named last changes fastest.
Arguments:
- field: float32 [32, 128, 128, 256], P(None, 'gz', 'gy'), may hold values from -6 to 6
- spectral_filter: float32 [2, 16, 16, 1024], P(None, None, 'gy', 'gz'), may hold values from -6 to 6
- depth_weight: float32 [32, 27], replicated, may hold values from -1.25 to 1.25
- point_weight: float32 [32, 32], replicated, may hold values from -1 to 1
- bias_vector: float32 [32], replicated, may hold values from -3 to 3
Outputs:
- layer_out: float32 [32, 128, 128, 256], P(None, 'gz', 'gy')
All inputs are finite; a program needn't handle non-finite values.
Results may differ from a plain program's by a relative error of at most 0.000057.
Values sent between devices are 32-bit elements; how exact they have to be, the bound alone decides.
A program may use at most 64 MiB of HBM per device.

v0:
```python
import math

import jax
import jax.numpy as jnp
from jax import lax
from jax.sharding import PartitionSpec as P

NX = 256
MX = 32
MY = 16
MZ = 16


HIGH = lax.Precision.HIGHEST


def cut_along(array, dim, size):
    shape = array.shape
    tiles = array.reshape(*shape[:dim], size, shape[dim] // size, *shape[dim + 1 :])
    return jnp.moveaxis(tiles, dim, 0)


def sum_at_owner(array, axis, dim):
    size = lax.axis_size(axis)
    tiles = lax.all_to_all(cut_along(array, dim, size), axis, 0, 0, tiled=True)
    return jnp.sum(tiles, axis=0)


def sent_to_all(array, axis):
    size = lax.axis_size(axis)
    return lax.all_to_all(
        jnp.broadcast_to(array[None], (size, *array.shape)), axis, 0, 0, tiled=True
    )


def joined_along(tiles, dim):
    shape = list(tiles.shape[1:])
    shape[dim] *= tiles.shape[0]
    return jnp.moveaxis(tiles, 0, dim).reshape(shape)


def collect(array, axis, dim):
    tiles = sent_to_all(array, axis)
    return joined_along(tiles, dim)


def with_halo(cells, sides, width):
    for axis, dim in sides:
        count = lax.axis_size(axis)
        head = lax.slice_in_dim(cells, 0, width, axis=dim)
        tail = lax.slice_in_dim(cells, cells.shape[dim] - width, cells.shape[dim], axis=dim)
        cells = jnp.concatenate(
            [
                lax.ppermute(tail, axis, [(i, (i + 1) % count) for i in range(count)]),
                cells,
                lax.ppermute(head, axis, [((i + 1) % count, i) for i in range(count)]),
            ],
            axis=dim,
        )
    return cells


def kept_freqs(count, total):
    series = jnp.arange(count, dtype=jnp.int32)
    return jnp.where(series < count // 2, series, total - count + series)


def phase_table(freqs, places, total):
    product = freqs[:, None] * places[None, :] % total
    angle = product.astype(jnp.float32) * (2.0 * math.pi / total)
    return (jnp.cos(angle), jnp.sin(angle))


def forward_pass(real_part, imag_part, cosine, sine, form):
    out_real = jnp.einsum(form, real_part, cosine, precision=HIGH) + jnp.einsum(
        form, imag_part, sine, precision=HIGH
    )
    out_imag = jnp.einsum(form, imag_part, cosine, precision=HIGH) - jnp.einsum(
        form, real_part, sine, precision=HIGH
    )
    return (out_real, out_imag)


def inverse_pass(real_part, imag_part, cosine, sine, form):
    out_real = jnp.einsum(form, real_part, cosine, precision=HIGH) - jnp.einsum(
        form, imag_part, sine, precision=HIGH
    )
    out_imag = jnp.einsum(form, real_part, sine, precision=HIGH) + jnp.einsum(
        form, imag_part, cosine, precision=HIGH
    )
    return (out_real, out_imag)


def apply_filter(values, gains):
    real_part = values[0] * gains[0] - values[1] * gains[1]
    imag_part = values[0] * gains[1] + values[1] * gains[0]
    return jnp.stack([real_part, imag_part], axis=0)


def body(field, spectral_filter, depth_weight, point_weight, bias_vector):
    chans = field.shape[0]
    z_local = field.shape[1]
    y_local = field.shape[2]
    z_total = z_local * lax.axis_size("gz")
    y_total = y_local * lax.axis_size("gy")
    y_places = lax.axis_index("gy") * y_local + jnp.arange(y_local, dtype=jnp.int32)
    x_freqs = jnp.arange(MX, dtype=jnp.int32)
    cos_x, sin_x = phase_table(x_freqs, jnp.arange(NX, dtype=jnp.int32), NX)
    cos_y, sin_y = phase_table(kept_freqs(MY, y_total), y_places, y_total)
    forward_scale = 1.0 / math.sqrt(float(NX) * y_total * z_total)
    x_table = jnp.stack([cos_x, -sin_x], axis=0)
    x_both = jnp.einsum("czyx,rkx->rzyck", field, x_table, precision=HIGH).reshape(
        2, z_local, y_local, chans * MX
    )
    cos_zf, sin_zf = phase_table(
        kept_freqs(MZ, z_total), jnp.arange(z_total, dtype=jnp.int32), z_total
    )
    columns = lax.all_to_all(x_both, "gz", split_axis=3, concat_axis=1, tiled=True)
    z_real, z_imag = forward_pass(columns[0], columns[1], cos_zf, sin_zf, "zyn,qz->qyn")
    y_real, y_imag = forward_pass(z_real, z_imag, cos_y, sin_y, "qyn,jy->qjn")
    partial_value = jnp.stack([y_real, y_imag], axis=0) * forward_scale
    owned = sum_at_owner(partial_value, "gy", 2)
    filtered = apply_filter(owned, spectral_filter)
    modes = collect(filtered, "gy", 2)
    b_real, b_imag = inverse_pass(modes[0], modes[1], cos_y, sin_y, "qjn,jy->qyn")
    c_real, c_imag = inverse_pass(b_real, b_imag, cos_zf, sin_zf, "qyn,qz->zyn")
    back = lax.all_to_all(
        jnp.stack([c_real, c_imag], axis=0), "gz", split_axis=1, concat_axis=3, tiled=True
    )
    back = back.reshape(2, z_local, y_local, chans, MX)
    weights = jnp.where(x_freqs == 0, 1.0, 2.0).astype(jnp.float32)[:, None]
    inverse_scale = 1.0 / math.sqrt(2.0 * MX * MY * MZ)
    inverse_table = jnp.stack([weights * cos_x, -(weights * sin_x)], axis=0) * inverse_scale
    spectral = jnp.einsum("rzyck,rkx->czyx", back, inverse_table, precision=HIGH)
    padded = with_halo(field, (("gz", 1), ("gy", 2)), 1)
    depth = jnp.zeros_like(field)
    for off_x in (-1, 0, 1):
        partial_sum = jnp.zeros_like(field)
        for off_z in (-1, 0, 1):
            for off_y in (-1, 0, 1):
                tap_index = (off_z + 1) * 9 + (off_y + 1) * 3 + (off_x + 1)
                window = padded[
                    :, 1 + off_z : 1 + off_z + z_local, 1 + off_y : 1 + off_y + y_local, :
                ]
                partial_sum = partial_sum + depth_weight[:, tap_index][:, None, None, None] * window
        depth = depth + jnp.roll(partial_sum, -off_x, axis=3)
    point = jnp.einsum("dc,czyx->dzyx", point_weight, depth, precision=HIGH)
    return jax.nn.gelu(spectral + point + bias_vector[:, None, None, None], approximate=False)


def solution(mesh):
    in_specs = (P(None, "gz", "gy", None), P(None, None, "gy", "gz"), P(), P(), P())
    out_specs = P(None, "gz", "gy", None)
    return jax.shard_map(body, mesh=mesh, in_specs=in_specs, out_specs=out_specs, check_vma=False)
```

profile of v0, /device:TPU:1, one launch (start us, length us, event | category | flops | bytes accessed | tf_op | source)
XLA Modules:
  0.0 128.3 jit_solution(6593610228321084818)
XLA Ops:
  0.2 4.0 %fusion.16 = f32[2,32,32,32]{3,1,2,0:T(8,128)S(1)} fusion(f32[32,1,32,256]{3,2,1,0:T(8,128)} %param.5, f32[1,32,256]{2,1,0:T(8,128)S(1)} %get-tuple-element.50, f32[1,32,256]{2,1,0:T(8,128)S(1)} %get-tuple-element.49), kind=kOutput, calls=%fused_computation.33 | convolution fusion | flops 201342976 | bytes 1376256 | tf_op jit(solution)/shard_map/czyx,rkx->rzyck/dot_general | solution.py:112
  4.2 0.8 copy.70
  5.0 1.7 %reshape.306 = f32[128,1,512]{2,1,0:T(1,128)} reshape(f32[1024,1,2,32]{3,2,1,0:T(2,128)S(1)} %bitcast.144) | data formatting | bytes 524288
  6.8 20.6 %all-to-all-start = ((f32[128,1,512]{2,1,0:T(1,128)}), f32[128,1,512]{2,1,0:T(1,128)S(1)}, u32[]{:S(2)}, u32[]{:S(2)}) async-start(f32[128,1,512]{2,1,0:T(1,128)} %reshape.306), calls=%async_computation | async-start | bytes 524288 | tf_op jit(solution)/shard_map/all_to_all | solution.py:118
  27.3 1.6 %copy.35 = f32[32,1,32,256]{3,0,2,1:T(8,128)} copy(f32[32,1,32,256]{3,2,1,0:T(8,128)S(1)} %copy-done.1) | data formatting | bytes 2097152 | tf_op args[0]
  28.9 2.8 %collective-permute-start.1 = (f32[32,1,32,256]{3,0,2,1:T(8,128)}, f32[32,1,32,256]{3,0,2,1:T(8,128)S(1)}, u32[]{:S(2)}, u32[]{:S(2)}) collective-permute-start(f32[32,1,32,256]{3,0,2,1:T(8,128)} %copy.35), channel_id=1, source_target_pairs={{4,0},{8,4},{12,8},{16,12},{20,16},{24,20},{28,24},{32,28},{36,32}... | collective-permute-start | bytes 3145736 | tf_op jit(solution)/shard_map/ppermute | solution.py:56
  31.7 2.8 %collective-permute-start = (f32[32,1,32,256]{3,0,2,1:T(8,128)}, f32[32,1,32,256]{3,0,2,1:T(8,128)S(1)}, u32[]{:S(2)}, u32[]{:S(2)}) collective-permute-start(f32[32,1,32,256]{3,0,2,1:T(8,128)} %copy.35), channel_id=1, source_target_pairs={{0,4},{4,8},{8,12},{12,16},{16,20},{20,24},{24,28},{28,32},{32,36}... | collective-permute-start | bytes 3145736 | tf_op jit(solution)/shard_map/ppermute | solution.py:54
  34.5 0.9 slice_reduce_fusion.1
  35.4 1.1 slice_reduce_fusion.17
  37.3 10.4 %all-to-all-done = f32[128,1,512]{2,1,0:T(1,128)S(1)} async-done(((f32[128,1,512]{2,1,0:T(1,128)}), f32[128,1,512]{2,1,0:T(1,128)S(1)}, u32[]{:S(2)}, u32[]{:S(2)}) %all-to-all-start) | async-done | bytes 262176 | tf_op jit(solution)/shard_map/all_to_all | solution.py:118
  49.0 2.2 %reduce.54 = f32[128,512]{1,0:T(8,128)S(1)} reduce(f32[128,1,512]{2,1,0:T(1,128)} %copy-done.4, f32[]{:T(128)} %broadcast.347), dimensions={1}, to_apply=%all_to_all.28.reduce_sub_computation | reduce | bytes 524292 | tf_op jit(solution)/shard_map/all_to_all | solution.py:118
  51.2 1.9 %reshape.307 = f32[1024,1,2,32]{3,2,1,0:T(2,128)} reshape(f32[128,512]{1,0:T(8,128)S(1)} %reduce.54) | data formatting | bytes 524288
  53.1 1.4 %copy.20 = f32[2,1,32,128,8]{3,2,4,1,0:T(8,128)S(1)} copy(f32[2,1,32,128,8]{2,0,4,3,1:T(2,128)} %bitcast.142) | data formatting | bytes 524288 | tf_op jit(solution)/shard_map/all_to_all | solution.py:118
  60.8 4.0 %all-to-all-start.1 = ((f32[4,1,1024]{2,1,0:T(1,128)}), f32[4,1,1024]{2,1,0:T(1,128)S(1)}, u32[]{:S(2)}, u32[]{:S(2)}) async-start(f32[4,1,1024]{2,1,0:T(1,128)} %reshape.308), calls=%async_computation.1 | async-start | bytes 32768 | tf_op jit(solution)/shard_map/all_to_all | solution.py:25
  64.8 1.1 constant_dynamic-update-slice_fusion.2
  65.9 1.6 %constant_dynamic-update-slice_fusion.1 = f32[32,3,32,256]{3,0,2,1:T(8,128)} fusion(f32[32,3,32,256]{3,0,2,1:T(8,128)} %constant_dynamic-update-slice_fusion.2, f32[32,1,32,256]{3,2,1,0:T(8,128)S(1)} %copy-done.1), kind=kLoop, calls=%fused_computation.155 | loop fusion | bytes 2097152
  67.5 1.1 constant_dynamic-update-slice_fusion
  70.7 3.9 %all-to-all-start.2 = ((f32[4,1,1024]{2,1,0:T(1,128)}), f32[4,1,1024]{2,1,0:T(1,128)S(1)}, u32[]{:S(2)}, u32[]{:S(2)}) async-start(f32[4,1,1024]{2,1,0:T(1,128)} %reshape.310), calls=%async_computation.2 | async-start | bytes 32768 | tf_op jit(solution)/shard_map/all_to_all | solution.py:31
  74.5 1.6 %fusion.191 = (f32[32,3,1,256]{3,0,2,1:T(8,128)}, f32[32,3,1,256]{3,0,2,1:T(8,128)}) fusion(f32[32,3,32,256]{3,0,2,1:T(8,128)} %constant_dynamic-update-slice_fusion), kind=kLoop, calls=%fused_computation.258 | loop fusion | bytes 393216 | tf_op jit(solution)/shard_map/slice | solution.py:50
  76.1 3.4 %collective-permute-start.2 = (f32[32,3,1,256]{3,0,2,1:T(8,128)}, f32[32,3,1,256]{3,0,2,1:T(8,128)S(1)}, u32[]{:S(2)}, u32[]{:S(2)}) collective-permute-start(f32[32,3,1,256]{3,0,2,1:T(8,128)} %get-tuple-element.40), channel_id=1, source_target_pairs={{0,1},{1,2},{2,3},{3,0},{4,5},{5,6},{6,7},{7,4},{8,9},{9,10},{10,1... | collective-permute-start | bytes 294920 | tf_op jit(solution)/shard_map/ppermute | solution.py:54
  79.5 3.1 %collective-permute-start.3 = (f32[32,3,1,256]{3,0,2,1:T(8,128)}, f32[32,3,1,256]{3,0,2,1:T(8,128)}, u32[]{:S(2)}, u32[]{:S(2)}) collective-permute-start(f32[32,3,1,256]{3,0,2,1:T(8,128)} %get-tuple-element.39), channel_id=1, source_target_pairs={{1,0},{2,1},{3,2},{0,3},{5,4},{6,5},{7,6},{4,7},{9,8},{10,9},{11,1... | collective-permute-start | bytes 294920 | tf_op jit(solution)/shard_map/ppermute | solution.py:56
  86.8 1.4 %copy.32 = f32[2,128,32,8]{2,3,0,1:T(8,128)} copy(f32[2,128,32,8]{1,2,3,0:T(8,128)S(1)} %pad_maximum_fusion.6) | data formatting | bytes 524288 | tf_op jit(solution)/shard_map/stack | solution.py:128
  88.2 2.4 %reshape.312 = f32[128,1,512]{2,1,0:T(1,128)} reshape(f32[128,2,8,32]{3,2,1,0:T(8,128)} %bitcast.143) | data formatting | bytes 524288
  90.6 9.8 %all-to-all-start.3 = ((f32[128,1,512]{2,1,0:T(1,128)}), f32[128,1,512]{2,1,0:T(1,128)S(1)}, u32[]{:S(2)}, u32[]{:S(2)}) async-start(f32[128,1,512]{2,1,0:T(1,128)} %reshape.312), calls=%async_computation.3 | async-start | bytes 524288 | tf_op jit(solution)/shard_map/all_to_all | solution.py:127
  100.5 4.2 %multiply_add_fusion = (f32[32,1,32,256]{3,0,2,1:T(8,128)S(1)}, f32[32,1,32,256]{3,0,2,1:T(8,128)S(1)}, f32[32,1,32,256]{3,0,2,1:T(8,128)S(1)}, f32[32,1,32,256]...) fusion(f32[32,1,32,256]{3,0,2,1:T(8,128)S(1)} %collective-permu, ...), kind=kLoop, calls=%fused_computation.48 | loop fusion | flops 6029312 | bytes 13829248 | tf_op jit(solution)/shard_map/add | solution.py:145
  105.4 1.4 %multiply_add_fusion.1 = f32[32,1,32,256]{3,0,2,1:T(8,128)S(1)} fusion(f32[32,1,32,256]{3,0,2,1:T(8,128)S(1)} %get-tuple-element.38, f32[32,1,32,256]{3,0,2,1:T(8,128)S(1)} %collective-permute-done.1, f32[32,1,32,256]{3,0,2,1:T(8,128)S(1)} %get-tuple-element.37, f32[32,1,32,256]{3,0,2,1:T(8,128)S(1)} %get-tuple-element.36, ...), kind=kLoop, calls=%fused_computation.66 | loop fusion | flops 4456448 | bytes 10486912 | tf_op jit(solution)/shard_map/add | solution.py:145
  107.1 3.6 %convolution_bitcast_fusion = f32[32,1,32,256]{3,0,2,1:T(8,128)} fusion(f32[32,1,32,255]{3,0,2,1:T(8,128)S(1)} %bitcast.141, f32[32,1,32,1]{3,0,2,1:T(8,128)S(1)} %slice.226, f32[32,1,32,1]{3,0,2,1:T(8,128)S(1)} %slice.229, f32[32,1,32,255]{3,0,2,1:T(8,128)S(1)} %slice.228, f32[32,1,32,256]{3,0,2,1:T(8,128)S(1)} %get-tuple-element.38, ...), kind=kOutput, calls=%fused_computation.1 | convolution fusion | flops 106168320 | bytes 12588160 | tf_op jit(solution)/shard_map/dc,czyx->dzyx/dot_general | solution.py:147
  110.7 10.1 %all-to-all-done.3 = f32[128,1,512]{2,1,0:T(1,128)S(1)} async-done(((f32[128,1,512]{2,1,0:T(1,128)}), f32[128,1,512]{2,1,0:T(1,128)S(1)}, u32[]{:S(2)}, u32[]{:S(2)}) %all-to-all-start.3) | async-done | bytes 262176 | tf_op jit(solution)/shard_map/all_to_all | solution.py:127
  120.8 1.2 reduce.57
  122.4 0.9 copy.34
  123.4 3.3 %fusion.7 = f32[32,1,32,256]{3,0,2,1:T(8,128)S(1)} fusion(f32[32,1,32,256]{3,0,2,1:T(8,128)S(1)} %copy-done.3, f32[2,32,32,32]{3,2,0,1:T(8,128)S(1)} %copy.34, f32[32]{0:T(128)S(1)} %copy-done.28, f32[1,32,256]{2,1,0:T(8,128)S(1)} %copy-done.7, f32[1,32,256]{2,1,0:T(8,128)S(1)} %copy-done.6), kind=kOutput, calls=%fused_computation.18 | convolution fusion | flops 218660864 | bytes 2424960 | tf_op jit(solution)/shard_map/rzyck,rkx->czyx/dot_general | solution.py:134
  126.7 1.6 %copy.41 = f32[32,1,32,256]{3,2,1,0:T(8,128)} copy(f32[32,1,32,256]{3,0,2,1:T(8,128)S(1)} %fusion.7) | data formatting | bytes 2097152 | tf_op jit(solution)/shard_map/mul | solution.py:148
  (109 shorter events, 15.8 us)
Async XLA Ops:
  0.0 107.0 %copy-start = (f32[32,32]{1,0:T(8,128)S(1)}, f32[32,32]{1,0:T(8,128)}, u32[]{:S(2)}) copy-start(f32[32,32]{1,0:T(8,128)} %param.8) | copy-start | bytes 12292
  0.0 27.3 %copy-start.1 = (f32[32,1,32,256]{3,2,1,0:T(8,128)S(1)}, f32[32,1,32,256]{3,2,1,0:T(8,128)}, u32[]{:S(2)}) copy-start(f32[32,1,32,256]{3,2,1,0:T(8,128)} %param.5) | copy-start | bytes 3145732
  4.2 30.3 %copy-start.2 = (f32[32,27]{1,0:T(8,128)S(1)}, f32[32,27]{1,0:T(8,128)}, u32[]{:S(2)}) copy-start(f32[32,27]{1,0:T(8,128)} %param.7) | copy-start | bytes 10372
  4.2 32.3 %copy-start.5 = (f32[2,16,4,8]{1,3,2,0:T(8,128)S(1)}, f32[2,16,4,8]{1,3,2,0:T(8,128)}, u32[]{:S(2)}) copy-start(f32[2,16,4,8]{1,3,2,0:T(8,128)} %param.6) | copy-start | bytes 12292
  6.8 41.0 %all-to-all-start = ((f32[128,1,512]{2,1,0:T(1,128)}), f32[128,1,512]{2,1,0:T(1,128)S(1)}, u32[]{:S(2)}, u32[]{:S(2)}) async-start(f32[128,1,512]{2,1,0:T(1,128)} %reshape.306), calls=%async_computation | async-start | bytes 524288 | tf_op jit(solution)/shard_map/all_to_all | solution.py:118
  28.9 38.6 %collective-permute-start.1 = (f32[32,1,32,256]{3,0,2,1:T(8,128)}, f32[32,1,32,256]{3,0,2,1:T(8,128)S(1)}, u32[]{:S(2)}, u32[]{:S(2)}) collective-permute-start(f32[32,1,32,256]{3,0,2,1:T(8,128)} %copy.35), channel_id=1, source_target_pairs={{4,0},{8,4},{12,8},{16,12},{20,16},{24,20},{28,24},{32,28},{36,32}... | collective-permute-start | bytes 3145736 | tf_op jit(solution)/shard_map/ppermute | solution.py:56
  31.7 33.1 %collective-permute-start = (f32[32,1,32,256]{3,0,2,1:T(8,128)}, f32[32,1,32,256]{3,0,2,1:T(8,128)S(1)}, u32[]{:S(2)}, u32[]{:S(2)}) collective-permute-start(f32[32,1,32,256]{3,0,2,1:T(8,128)} %copy.35), channel_id=1, source_target_pairs={{0,4},{4,8},{8,12},{12,16},{16,20},{20,24},{24,28},{28,32},{32,36}... | collective-permute-start | bytes 3145736 | tf_op jit(solution)/shard_map/ppermute | solution.py:54
  47.8 0.7 copy-start.4
  60.8 8.2 %all-to-all-start.1 = ((f32[4,1,1024]{2,1,0:T(1,128)}), f32[4,1,1024]{2,1,0:T(1,128)S(1)}, u32[]{:S(2)}, u32[]{:S(2)}) async-start(f32[4,1,1024]{2,1,0:T(1,128)} %reshape.308), calls=%async_computation.1 | async-start | bytes 32768 | tf_op jit(solution)/shard_map/all_to_all | solution.py:25
  70.7 12.0 %all-to-all-start.2 = ((f32[4,1,1024]{2,1,0:T(1,128)}), f32[4,1,1024]{2,1,0:T(1,128)S(1)}, u32[]{:S(2)}, u32[]{:S(2)}) async-start(f32[4,1,1024]{2,1,0:T(1,128)} %reshape.310), calls=%async_computation.2 | async-start | bytes 32768 | tf_op jit(solution)/shard_map/all_to_all | solution.py:31
  76.1 24.2 %collective-permute-start.2 = (f32[32,3,1,256]{3,0,2,1:T(8,128)}, f32[32,3,1,256]{3,0,2,1:T(8,128)S(1)}, u32[]{:S(2)}, u32[]{:S(2)}) collective-permute-start(f32[32,3,1,256]{3,0,2,1:T(8,128)} %get-tuple-element.40), channel_id=1, source_target_pairs={{0,1},{1,2},{2,3},{3,0},{4,5},{5,6},{6,7},{7,4},{8,9},{9,10},{10,1... | collective-permute-start | bytes 294920 | tf_op jit(solution)/shard_map/ppermute | solution.py:54
  79.5 20.9 %collective-permute-start.3 = (f32[32,3,1,256]{3,0,2,1:T(8,128)}, f32[32,3,1,256]{3,0,2,1:T(8,128)}, u32[]{:S(2)}, u32[]{:S(2)}) collective-permute-start(f32[32,3,1,256]{3,0,2,1:T(8,128)} %get-tuple-element.39), channel_id=1, source_target_pairs={{1,0},{2,1},{3,2},{0,3},{5,4},{6,5},{7,6},{4,7},{9,8},{10,9},{11,1... | collective-permute-start | bytes 294920 | tf_op jit(solution)/shard_map/ppermute | solution.py:56
  83.3 17.1 %copy-start.24 = (f32[32]{0:T(128)S(1)}, f32[32]{0:T(128)}, u32[]{:S(2)}) copy-start(f32[32]{0:T(128)} %get-tuple-element.24) | copy-start | bytes 388
  83.4 17.1 %copy-start.25 = (f32[32]{0:T(128)S(1)}, f32[32]{0:T(128)}, u32[]{:S(2)}) copy-start(f32[32]{0:T(128)} %get-tuple-element.31) | copy-start | bytes 388
  83.4 17.1 %copy-start.26 = (f32[32]{0:T(128)S(1)}, f32[32]{0:T(128)}, u32[]{:S(2)}) copy-start(f32[32]{0:T(128)} %get-tuple-element.6) | copy-start | bytes 388
  83.4 17.1 %copy-start.27 = (f32[32]{0:T(128)S(1)}, f32[32]{0:T(128)}, u32[]{:S(2)}) copy-start(f32[32]{0:T(128)} %get-tuple-element.7) | copy-start | bytes 388
  90.6 30.2 %all-to-all-start.3 = ((f32[128,1,512]{2,1,0:T(1,128)}), f32[128,1,512]{2,1,0:T(1,128)S(1)}, u32[]{:S(2)}, u32[]{:S(2)}) async-start(f32[128,1,512]{2,1,0:T(1,128)} %reshape.312), calls=%async_computation.3 | async-start | bytes 524288 | tf_op jit(solution)/shard_map/all_to_all | solution.py:127
  104.7 0.7 copy-start.10
  104.7 0.7 copy-start.23
  105.4 1.7 %copy-start.12 = (f32[32]{0:T(128)S(1)}, f32[32]{0:T(128)}, u32[]{:S(2)}) copy-start(f32[32]{0:T(128)} %get-tuple-element.5) | copy-start | bytes 388
  105.4 1.7 %copy-start.13 = (f32[32]{0:T(128)S(1)}, f32[32]{0:T(128)}, u32[]{:S(2)}) copy-start(f32[32]{0:T(128)} %get-tuple-element.13) | copy-start | bytes 388
  105.4 1.7 %copy-start.14 = (f32[32]{0:T(128)S(1)}, f32[32]{0:T(128)}, u32[]{:S(2)}) copy-start(f32[32]{0:T(128)} %get-tuple-element.14) | copy-start | bytes 388
  105.4 1.7 %copy-start.15 = (f32[32]{0:T(128)S(1)}, f32[32]{0:T(128)}, u32[]{:S(2)}) copy-start(f32[32]{0:T(128)} %get-tuple-element.15) | copy-start | bytes 388
  105.4 1.7 %copy-start.16 = (f32[32]{0:T(128)S(1)}, f32[32]{0:T(128)}, u32[]{:S(2)}) copy-start(f32[32]{0:T(128)} %get-tuple-element.16) | copy-start | bytes 388
  105.4 1.7 %copy-start.17 = (f32[32]{0:T(128)S(1)}, f32[32]{0:T(128)}, u32[]{:S(2)}) copy-start(f32[32]{0:T(128)} %get-tuple-element.17) | copy-start | bytes 388
  105.4 1.7 %copy-start.18 = (f32[32]{0:T(128)S(1)}, f32[32]{0:T(128)}, u32[]{:S(2)}) copy-start(f32[32]{0:T(128)} %get-tuple-element.18) | copy-start | bytes 388
  105.4 1.7 %copy-start.19 = (f32[32]{0:T(128)S(1)}, f32[32]{0:T(128)}, u32[]{:S(2)}) copy-start(f32[32]{0:T(128)} %get-tuple-element.19) | copy-start | bytes 388
  105.4 1.7 %copy-start.20 = (f32[32]{0:T(128)S(1)}, f32[32]{0:T(128)}, u32[]{:S(2)}) copy-start(f32[32]{0:T(128)} %get-tuple-element.20) | copy-start | bytes 388
  110.7 12.7 %copy-start.3 = (f32[32,1,32,256]{3,0,2,1:T(8,128)S(1)}, f32[32,1,32,256]{3,0,2,1:T(8,128)}, u32[]{:S(2)}) copy-start(f32[32,1,32,256]{3,0,2,1:T(8,128)} %convolution_bitcast_fusion) | copy-start | bytes 3145732
  110.7 12.7 %copy-start.6 = (f32[1,32,256]{2,1,0:T(8,128)S(1)}, f32[1,32,256]{2,1,0:T(8,128)}, u32[]{:S(2)}) copy-start(f32[1,32,256]{2,1,0:T(8,128)} %get-tuple-element.47) | copy-start | bytes 98308
  110.7 12.7 %copy-start.7 = (f32[1,32,256]{2,1,0:T(8,128)S(1)}, f32[1,32,256]{2,1,0:T(8,128)}, u32[]{:S(2)}) copy-start(f32[1,32,256]{2,1,0:T(8,128)} %get-tuple-element.48) | copy-start | bytes 98308
  110.7 12.7 %copy-start.28 = (f32[32]{0:T(128)S(1)}, f32[32]{0:T(128)}, u32[]{:S(2)}) copy-start(f32[32]{0:T(128)} %param.9) | copy-start | bytes 388
  (5 other events, 3.1 us)
where the time goes:
time: 130 us; the launch traced here: 128 us
  starting transfers between devices  50.3 us (39%)
  local copies, waits for them, and re-layouts  25.6 us (20%)
  waiting for transfers between devices  20.9 us (16%)
  matrix products  19.4 us (15%)
  other arithmetic  11.5 us (9%)
    all_to_all x1, starting transfers between devices, body(): lax.all_to_all(x_both, 'gz', split_axis=3, concat_axis=1, tiled=True)  20.6 us
    unnamed x70, local copies, waits for them, and re-layouts  13.4 us
    all_to_all x1, waiting for transfers between devices, body(): lax.all_to_all(x_both, 'gz', split_axis=3, concat_axis=1, tiled=True)  10.4 us
    all_to_all x1, waiting for transfers between devices, body(): lax.all_to_all(jnp.stack([c_real, c_imag], axis=0), 'gz', split_axis=1, c...  10.1 us
    all_to_all x1, starting transfers between devices, body(): lax.all_to_all(jnp.stack([c_real, c_imag], axis=0), 'gz', split_axis=1, c...  9.78 us
    ppermute x2, starting transfers between devices, with_halo(): lax.ppermute(tail, axis, [(i, (i + 1) % count) for i in range(count)])  6.12 us
    ppermute x2, starting transfers between devices, with_halo(): lax.ppermute(head, axis, [((i + 1) % count, i) for i in range(count)])  5.92 us
    add x2, other arithmetic, body(): partial_sum + depth_weight[:, tap_index][:, None, None, None] * window  5.59 us
  transfers between devices with their start and end apart: 8, of which 3 were waited for; matrix products, arithmetic and copies ran while one was open for 31% of the time, Pallas kernels for 0%

commit v1 on v0

v1 whole, which is shorter than its diff:
```python
import functools

import jax
import jax.numpy as jnp
import ml_dtypes
import numpy as np
from jax import lax
from jax.experimental import pallas as pl
from jax.experimental.pallas import tpu as pltpu
from jax.sharding import PartitionSpec as P

C = 32
NX = 256
NY = 128
NZ = 128
MX = 32
MY = 16
MZ = 16
GY = 4
ZC = 16
W = 8
YL = NY // GY
MESH = pl.DeviceIdType.MESH
F32 = jnp.float32
BF16 = jnp.bfloat16
VMEM = pltpu.VMEM
DMA = pltpu.SemaphoreType.DMA


def halves(table):
    high = table.astype(ml_dtypes.bfloat16)
    low = (table - high.astype(np.float64)).astype(ml_dtypes.bfloat16)
    return high, low


def kept(count, total):
    series = np.arange(count)
    return np.where(series < count // 2, series, total - count + series)


def make_tables():
    tables = {}
    angle = 2 * np.pi * (np.arange(NX)[:, None] * np.arange(MX)[None, :] % NX) / NX
    cos = np.cos(angle).reshape(NX, 4, 8)
    sin = np.sin(angle).reshape(NX, 4, 8)
    plain = np.stack([cos, -sin], axis=2).reshape(NX, 64)
    swapped = np.stack([-sin, -cos], axis=2).reshape(NX, 64)
    zero = np.zeros_like(plain)
    tx = np.stack(
        [
            np.concatenate([plain, zero, swapped, zero], axis=1),
            np.concatenate([zero, plain, zero, swapped], axis=1),
        ]
    )
    tables["tx"] = np.stack(halves(tx))
    places = np.arange(NY)
    angle = 2 * np.pi * (kept(MY, NY)[:, None] * places[None, :] % NY) / NY
    parts = []
    for value in (np.cos(angle), np.sin(angle)):
        parts.extend(part.astype(np.float32) for part in halves(value))
    stack = np.stack(parts)
    mine = stack.reshape(4, MY, GY, YL).transpose(2, 0, 1, 3)
    tables["ty"] = np.tile(mine, (1, 1, 1, 8))
    tables["tyi"] = np.repeat(mine.transpose(0, 1, 3, 2), 8, axis=3)
    angle = 2 * np.pi * (kept(MZ, NZ)[:, None] * np.arange(NZ)[None, :] % NZ) / NZ
    high, low = halves(np.concatenate([np.cos(angle), np.sin(angle)], axis=0))
    tables["tz"] = np.concatenate([high, low], axis=0)
    scale = (NX * NY * NZ) ** -0.5 * (2.0 * MX * MY * MZ) ** -0.5
    both = np.concatenate([np.cos(angle), np.sin(angle)], axis=0).T * scale
    high, low = halves(both)
    tables["tzi"] = np.concatenate(
        [high.reshape(ZC, W, 32), low.reshape(ZC, W, 32)], axis=1
    ).astype(np.float32)
    row = np.arange(128)[:, None]
    col = np.arange(512)[None, :]
    tables["te"] = (
        (row // 32 == col // 128) & (row % 32 // 8 == col % 64 // 16) & (row % 8 == col % 8)
    ).astype(ml_dtypes.bfloat16)
    weight = np.where(np.arange(MX) == 0, 1.0, 2.0)[:, None]
    angle = 2 * np.pi * (np.arange(MX)[:, None] * np.arange(NX)[None, :] % NX) / NX
    cos = (weight * np.cos(angle)).reshape(4, 8, NX)
    sin = (weight * np.sin(angle)).reshape(4, 8, NX)
    from_c = np.stack([cos, -sin], axis=1).reshape(64, NX)
    from_s = np.stack([-sin, -cos], axis=1).reshape(64, NX)
    zero = np.zeros_like(from_c)
    txi = np.block([[from_c, zero], [zero, from_c], [from_s, zero], [zero, from_s]])
    tables["txi"] = np.stack(halves(txi))
    return tables


TABLES = make_tables()


def split(value):
    high = value.astype(BF16)
    return high, (value - high.astype(F32)).astype(BF16)


def dot(left, right):
    return jnp.dot(left, right, preferred_element_type=F32)


def iota(shape, dim):
    return lax.broadcasted_iota(jnp.int32, shape, dim)


def swapped(value):
    pieces = []
    for k in range(value.shape[1] // 128):
        piece = value[:, k * 128 : (k + 1) * 128]
        real_lane = iota(piece.shape, 1) % 16 < 8
        pieces.append(jnp.where(real_lane, pltpu.roll(piece, 120, 1), -pltpu.roll(piece, 8, 1)))
    return jnp.concatenate(pieces, axis=1)


def moved(value, blocks):
    return value if blocks % 8 == 0 else pltpu.roll(value, blocks % 8 * 16, 1)


def wide_kernel(
    field3, filt, depth_w, point_w, tx, ty, tz, tzi, te,
    tiles_out, point_out,
    fv, pad, edge, hrow, xh, xl, yout, send1, recv1, tmp, send2, agbuf, gains,
    fscr, ftile, fbuf, tmp3, depth, pacc,
    ld_sem, s1, r1, sf, rf, sh, rh, sz, rz, s2, r2, s3, r3, so,
):
    gz = lax.axis_index("gz")
    gy = lax.axis_index("gy")
    zc = gz // W
    w = gz % W
    core = gz % 2
    me = gy * W + w

    def plane_peer(i):
        t = (me + i) % 32
        return (zc * W + t % W, t // W), t

    def ring_peer(i):
        return ((zc + i) % ZC) * W + w

    def halo_peer(dz, dy):
        return ((gz + NZ + dz) % NZ, (gy + GY + dy) % GY)

    barrier = pltpu.get_barrier_semaphore()

    def signal(target):
        pl.semaphore_signal(barrier, inc=1, device_id=target, device_id_type=MESH)

    def greet_ring(i, carry):
        signal((ring_peer(i), gy))
        return carry

    def greet_plane(i, carry):
        signal(plane_peer(i)[0])
        return carry

    lax.fori_loop(1, ZC, greet_ring, 0)
    for dz in (-1, 1):
        for dy in (-1, 0, 1):
            signal(halo_peer(dz, dy))
    lax.fori_loop(1, 32, greet_plane, 0)

    load = pltpu.make_async_copy(field3, fv, ld_sem.at[0])
    load.start()
    load_mid = pltpu.make_async_copy(field3, pad.at[1, :, 8:40, :], ld_sem.at[1])
    load_mid.start()

    fscr[...] = jnp.zeros_like(fscr)
    fscr[:, 0:8] = filt[...]
    tile = jnp.zeros((8, 128), F32)
    for b in range(4):
        for ky in range(4):
            piece = fscr[pl.ds(b * 32 + ky, 8, stride=4), :]
            shift = b * 32 + ky * 8
            tile = tile + (piece if shift == 0 else pltpu.roll(piece, shift, 1))
    ftile[...] = tile

    load.wait()
    for side, row in ((0, YL - 1), (1, 0)):
        edge[side] = fv[:, row, :]

    for p in range(2):
        total = None
        for ml in range(2):
            g = 2 * ml + p
            rows = jnp.concatenate(
                [fv[4 * s + g] for s in range(8)], axis=0
            )
            high, low = split(rows)
            value = dot(high, tx[0, ml]) + dot(low, tx[0, ml]) + dot(high, tx[1, ml])
            total = value if total is None else total + value
        high, low = split(total)
        for part in range(2):
            xh[part * 256 : (part + 1) * 256, p * 128 : (p + 1) * 128] = high[:, part * 128 : (part + 1) * 128]
            xl[part * 256 : (part + 1) * 256, p * 128 : (p + 1) * 128] = low[:, part * 128 : (part + 1) * 128]
    same = iota((MY, 8, 256), 1) == iota((MY, 8, 256), 2) // YL

    def spread(which):
        base = ty[gy, which]
        wide = jnp.where(same, jnp.broadcast_to(base[:, None, :], (MY, 8, 256)), 0.0)
        return wide.reshape(128, 256).astype(BF16)

    y_high = jnp.concatenate([spread(0), spread(2)], axis=1)
    y_low = jnp.concatenate([spread(1), spread(3)], axis=1)
    y_both = jnp.concatenate([y_high, y_low], axis=0)
    result = dot(y_both, xh[...]) + dot(y_both, xl[...])
    yout[...] = result[0:128] + result[128:256]
    block = iota((8, 128), 1) // 16 % 4
    for p in range(2):
        for q in range(4):
            quad = [
                yout[(q * 4 + ky) * 8 : (q * 4 + ky + 1) * 8, p * 128 : (p + 1) * 128]
                for ky in range(4)
            ]
            for kxb in range(4):
                out = moved(quad[0], 0 - kxb)
                for ky in range(1, 4):
                    out = jnp.where(block == ky, moved(quad[ky], ky - kxb), out)
                send1[q * 8 + p * 4 + kxb] = out

    pl.semaphore_wait(barrier, 15 + 6 + 31)

    def copy1(i):
        target, t = plane_peer(i)
        return pltpu.make_async_remote_copy(
            send1.at[t], recv1.at[me], s1, r1, device_id=target, device_id_type=MESH
        )

    def start1(i, carry):
        copy1(i).start()
        return carry

    lax.fori_loop(1, 32, start1, 0)
    own1 = pltpu.make_async_copy(send1.at[me], recv1.at[me], r1)
    own1.start()

    def copyf(i):
        return pltpu.make_async_remote_copy(
            ftile, fbuf.at[zc], sf, rf, device_id=(ring_peer(i), gy), device_id_type=MESH
        )

    def startf(i, carry):
        copyf(i).start()
        return carry

    def copy_row(dz, side):
        dy = 1 if side == 0 else -1
        slot = (1 - dz) * 2 + side
        return pltpu.make_async_remote_copy(
            edge.at[side], hrow.at[slot], sh, rh.at[0 if dz == 0 else 1],
            device_id=halo_peer(dz, dy), device_id_type=MESH,
        )

    def copy_plane(dz):
        return pltpu.make_async_remote_copy(
            field3, pad.at[1 - dz, :, 8:40, :], sz, rz.at[1 - dz],
            device_id=halo_peer(dz, 0), device_id_type=MESH,
        )

    for side in range(2):
        copy_row(0, side).start()
    for dz in (-1, 1):
        copy_plane(dz).start()
    for dz in (-1, 1):
        for side in range(2):
            copy_row(dz, side).start()
    lax.fori_loop(1, ZC, startf, 0)
    own_f = pltpu.make_async_copy(ftile, fbuf.at[zc], rf)
    own_f.start()

    def put_rows(plane, slot):
        pad[plane, :, 7, :] = hrow[slot]
        pad[plane, :, 40, :] = hrow[slot + 1]

    def conv(plane, first):
        def channel(c, carry):
            sums = [None, None, None]
            for b in range(3):
                window = pad[plane, c, 7 + b : 39 + b, :]
                for e in range(3):
                    term = depth_w[c, plane * 9 + b * 3 + e] * window
                    sums[e] = term if sums[e] is None else sums[e] + term
            value = sums[1] + pltpu.roll(sums[0], 1, 1) + pltpu.roll(sums[2], NX - 1, 1)
            depth[c] = value if first else depth[c] + value
            return carry

        lax.fori_loop(0, C, channel, 0)

    load_mid.wait()

    def wait_rows(index, count):
        part = hrow.at[0:count]
        pltpu.make_async_copy(part, part, rh.at[index]).wait()

    wait_rows(0, 2)
    put_rows(1, 2)
    conv(1, True)

    pltpu.make_async_copy(recv1, recv1, r1).wait()
    for k in range(W):
        tmp[k * 8 : (k + 1) * 8, :] = (recv1[k] + recv1[8 + k]) + (recv1[16 + k] + recv1[24 + k])
    for s in range(8):
        send2[:, s * 128 : (s + 1) * 128] = tmp[pl.ds(s, 8, stride=8), :]

    def far_first(k):
        return 8 + (k + 1) // 2 * (2 * (k % 2) - 1)

    def copy2(k):
        return pltpu.make_async_remote_copy(
            send2, agbuf.at[zc], s2, r2, device_id=(ring_peer(far_first(k)), gy), device_id_type=MESH
        )

    def start2(k, carry):
        copy2(k).start()
        return carry

    lax.fori_loop(0, ZC - 1, start2, 0)
    own2 = pltpu.make_async_copy(send2, agbuf.at[zc], r2)
    own2.start()

    pltpu.make_async_copy(fbuf, fbuf, rf).wait()
    raw = fbuf[...].reshape(128, 128)
    high = raw.astype(BF16)
    rest = raw - high.astype(F32)
    mid = rest.astype(BF16)
    low = (rest - mid.astype(F32)).astype(BF16)
    wide = dot(high, te[...]) + dot(mid, te[...]) + dot(low, te[...])
    lower = iota((8, 128), 1) < 64
    for part in range(2):
        for h in range(2):
            lanes = slice((part * 2 + h) * 128, (part * 2 + h + 1) * 128)
            for s in range(8):
                gains[part, h * 8 : (h + 1) * 8, s * 128 : (s + 1) * 128] = jnp.where(
                    lower, wide[s * 16 : s * 16 + 8, lanes], wide[s * 16 + 8 : s * 16 + 16, lanes]
                )

    wait_rows(1, 4)
    near = jnp.where(core == 0, 2, 0)
    far = 2 - near
    pltpu.make_async_copy(field3, pad.at[near, :, 8:40, :], rz.at[near]).wait()
    put_rows(near, near * 2)
    conv(near, False)

    pltpu.make_async_copy(agbuf, agbuf, r2).wait()
    a_high, a_low = split(agbuf[...].reshape(NZ, 1024))
    both = dot(tz[...], a_high) + dot(tz[...], a_low)
    modes = both[0:16] + both[32:48] + swapped(both[16:32] + both[48:64])
    filtered = modes * gains[0] - swapped(modes) * gains[1]
    stacked = jnp.concatenate([filtered, -swapped(filtered)], axis=0)
    f_high, f_low = split(stacked)
    table = tzi[zc].astype(BF16)
    both = dot(table, f_high) + dot(table, f_low)
    back = both[0:8] + both[8:16]
    for s in range(8):
        tmp3[pl.ds(s, 8, stride=8), :] = back[:, s * 128 : (s + 1) * 128]

    def copy3(i):
        target, t = plane_peer(i)
        return pltpu.make_async_remote_copy(
            tmp3.at[pl.ds(pl.multiple_of(t % W * 8, 8), 8), :], tiles_out.at[w * 4 + gy], s3, r3,
            device_id=target, device_id_type=MESH,
        )

    def start3(i, carry):
        copy3(i).start()
        return carry

    lax.fori_loop(1, 32, start3, 0)
    own3 = pltpu.make_async_copy(
        tmp3.at[pl.ds(pl.multiple_of(w * 8, 8), 8), :], tiles_out.at[w * 4 + gy], r3
    )
    own3.start()

    pltpu.make_async_copy(field3, pad.at[far, :, 8:40, :], rz.at[far]).wait()
    put_rows(far, far * 2)
    conv(far, False)

    grow = (iota((256, C), 0) // 8 == iota((256, C), 1)).astype(F32).astype(BF16)
    grow_t = (iota((C, 256), 1) // 8 == iota((C, 256), 0)).astype(F32).astype(BF16)
    diagonal = iota((256, 256), 0) % 8 == iota((256, 256), 1) % 8
    mixers = []
    for part in split(point_w[...]):
        tall = dot(grow, part).astype(BF16)
        mixers.append(jnp.where(diagonal, dot(tall, grow_t), 0.0).astype(BF16))
    for k in range(YL // 8):
        d_high, d_low = split(depth[:, k * 8 : (k + 1) * 8, :].reshape(256, NX))
        value = dot(mixers[0], d_high) + dot(mixers[0], d_low) + dot(mixers[1], d_high)
        pacc[:, k * 8 : (k + 1) * 8, :] = value.reshape(C, 8, NX)
    put = pltpu.make_async_copy(pacc, point_out, so)
    put.start()

    pltpu.make_async_copy(tiles_out, tiles_out, r3).wait()
    put.wait()

    def done1(i, carry):
        copy1(i).wait_send()
        copy3(i).wait_send()
        return carry

    def done2(k, carry):
        copy2(k).wait_send()
        return carry

    def donef(i, carry):
        copyf(i).wait_send()
        return carry

    lax.fori_loop(1, 32, done1, 0)
    lax.fori_loop(0, ZC - 1, done2, 0)
    lax.fori_loop(1, ZC, donef, 0)
    for dz in (-1, 0, 1):
        for side in range(2):
            copy_row(dz, side).wait_send()
    for dz in (-1, 1):
        copy_plane(dz).wait_send()


def last_kernel(tiles, point, bias, tyi, txi, out, yh, yl):
    step = pl.program_id(0)
    gy = lax.axis_index("gy")

    @pl.when(step == 0)
    def _():
        block = iota((8, 128), 1) // 16 % 4
        columns = []
        for p in range(2):
            rows = []
            for ky in range(MY):
                q, k4 = ky // 4, ky % 4
                value = moved(tiles[p * 16 + q], 0 - k4)
                for kxb in range(1, 4):
                    value = jnp.where(block == kxb, moved(tiles[(p * 4 + kxb) * 4 + q], kxb - k4), value)
                rows.append(value)
            columns.append(jnp.concatenate(rows, axis=0))
        r_high, r_low = split(jnp.concatenate(columns, axis=1))
        same = iota((8, YL, 128), 0) == iota((8, YL, 128), 2) % 8

        def spread(which):
            base = tyi[gy, which]
            wide = jnp.where(same, jnp.broadcast_to(base[None], (8, YL, 128)), 0.0)
            return wide.reshape(256, 128).astype(BF16)

        t_high = jnp.concatenate([spread(0), spread(2)], axis=0)
        t_low = jnp.concatenate([spread(1), spread(3)], axis=0)
        value = dot(t_high, r_high) + dot(t_high, r_low) + dot(t_low, r_high)
        high, low = split(value)
        yh[...] = high
        yl[...] = low

    def gathered(ref):
        start = pl.multiple_of(step * 64, 64)
        real = ref[pl.ds(start, 64), :]
        imag = ref[pl.ds(256 + start, 64), :]
        return jnp.concatenate(
            [
                jnp.concatenate([real[:, p * 128 : (p + 1) * 128], imag[:, p * 128 : (p + 1) * 128]], axis=1)
                for p in range(2)
            ],
            axis=0,
        )

    high, low = gathered(yh), gathered(yl)
    spectral = dot(high, txi[0]) + dot(low, txi[0]) + dot(high, txi[1])
    for p in range(2):
        for sl in range(2):
            for ml in range(2):
                ch = 4 * sl + 2 * ml + p
                value = spectral[p * 64 + sl * 32 : p * 64 + (sl + 1) * 32, ml * 256 : (ml + 1) * 256]
                value = value + point[ch] + bias[step * 8 + ch]
                out[ch] = 0.5 * value * (1.0 + lax.erf(value * (0.5**0.5)))


def body(field, spectral_filter, depth_weight, point_weight, bias_vector):
    field3 = field.reshape(C, YL, NX)
    filt = spectral_filter.reshape(128, 8)
    const = {name: jnp.asarray(value) for name, value in TABLES.items()}
    vmem = pl.BlockSpec(memory_space=pltpu.VMEM)
    smem = pl.BlockSpec(memory_space=pltpu.SMEM)
    hbm = pl.BlockSpec(memory_space=pl.ANY)
    tiles, point = pl.pallas_call(
        wide_kernel,
        name="wide",
        out_shape=(
            jax.ShapeDtypeStruct((32, 8, 128), F32),
            jax.ShapeDtypeStruct((C, YL, NX), F32),
        ),
        in_specs=[hbm, vmem, smem, vmem, vmem, vmem, vmem, vmem, vmem],
        out_specs=(hbm, hbm),
        scratch_shapes=[
            VMEM((C, YL, NX), F32),
            VMEM((3, C, 48, NX), F32),
            VMEM((2, C, NX), F32),
            VMEM((6, C, NX), F32),
            VMEM((512, 256), BF16),
            VMEM((512, 256), BF16),
            VMEM((128, 256), F32),
            VMEM((32, 8, 128), F32),
            VMEM((32, 8, 128), F32),
            VMEM((64, 128), F32),
            VMEM((8, 1024), F32),
            VMEM((ZC, 8, 1024), F32),
            VMEM((2, 16, 1024), F32),
            VMEM((128, 128), F32),
            VMEM((8, 128), F32),
            VMEM((ZC, 8, 128), F32),
            VMEM((64, 128), F32),
            VMEM((C, YL, NX), F32),
            VMEM((C, YL, NX), F32),
            DMA((2,)), DMA, DMA, DMA, DMA, DMA, DMA((2,)), DMA, DMA((3,)), DMA, DMA, DMA, DMA, DMA,
        ],
        compiler_params=pltpu.CompilerParams(
            collective_id=0, has_side_effects=True, vmem_limit_bytes=40 * 1024 * 1024
        ),
    )(
        field3, filt, depth_weight, point_weight,
        const["tx"], const["ty"], const["tz"], const["tzi"], const["te"],
    )
    out = pl.pallas_call(
        last_kernel,
        name="last",
        out_shape=jax.ShapeDtypeStruct((C, YL, NX), F32),
        grid=(4,),
        in_specs=[
            vmem,
            pl.BlockSpec((8, YL, NX), lambda i: (i, 0, 0)),
            smem,
            vmem,
            vmem,
        ],
        out_specs=pl.BlockSpec((8, YL, NX), lambda i: (i, 0, 0)),
        scratch_shapes=[VMEM((512, 256), BF16), VMEM((512, 256), BF16)],
        compiler_params=pltpu.CompilerParams(dimension_semantics=("arbitrary",)),
    )(tiles, point, bias_vector, const["tyi"], const["txi"])
    return out.reshape(C, 1, YL, NX)


def solution(mesh):
    in_specs = (P(None, "gz", "gy", None), P(None, None, "gy", "gz"), P(), P(), P())
    out_specs = P(None, "gz", "gy", None)
    return jax.shard_map(body, mesh=mesh, in_specs=in_specs, out_specs=out_specs, check_vma=False)
```

time: 130 us -> 75.5 us (0.58); the launches traced: 128 us -> 75.1 us
  Pallas kernels: 0 us -> 67.5 us
  starting transfers between devices: 50.3 us -> 0 us
  waiting for transfers between devices: 20.9 us -> 0 us
  matrix products: 19.4 us -> 0 us
  local copies, waits for them, and re-layouts: 25.6 us -> 7.53 us
  other arithmetic: 11.5 us -> 0 us
    pallas_call x0 -> x2, Pallas kernels: none -> 67.5 us  [the longest x1 62.8 us: body(): pl.pallas_call(wide_kernel, name='wide', out_shape=(jax.ShapeDtypeStruct(...]
    all_to_all x4 -> x0, starting transfers between devices: 38.2 us -> none  [the longest x1 20.6 us: body(): lax.all_to_all(x_both, 'gz', split_axis=3, concat_axis=1, tiled=True)]
    all_to_all x4 -> x0, waiting for transfers between devices: 20.9 us -> none  [the longest x1 10.4 us: body(): lax.all_to_all(x_both, 'gz', split_axis=3, concat_axis=1, tiled=True)]
    dot_general x19 -> x0, matrix products: 19.4 us -> none  [the longest x1 4.01 us: body(): jnp.einsum('czyx,rkx->rzyck', field, x_table, precision=HIGH)]
    ppermute x4 -> x0, starting transfers between devices: 12 us -> none  [the longest x2 6.12 us: with_halo(): lax.ppermute(tail, axis, [(i, (i + 1) % count) for i in range(count)])]
    unnamed x70 -> x21, local copies, waits for them, and re-layouts: 13.4 us -> 7.53 us
    add x3 -> x0, other arithmetic: 5.6 us -> none  [the longest x2 5.59 us: body(): partial_sum + depth_weight[:, tap_index][:, None, None, None] * window]
    all_to_all x4 -> x0, other arithmetic: 4.79 us -> none  [the longest x1 2.2 us: body(): lax.all_to_all(x_both, 'gz', split_axis=3, concat_axis=1, tiled=True)]
  transfers between devices with their start and end apart: 8 -> 0, of which waited for: 3 -> 0; matrix products, arithmetic and copies ran while one was open for 31% -> 0% of each run, Pallas kernels for 0% -> 0%
where the time goes in v1:
time: 75.5 us; the launch traced here: 75.1 us
  Pallas kernels  67.5 us (89%)
  local copies, waits for them, and re-layouts  7.53 us (10%)
    pallas_call x1, Pallas kernels, body(): pl.pallas_call(wide_kernel, name='wide', out_shape=(jax.ShapeDtypeStruct(...  62.8 us
    unnamed x21, local copies, waits for them, and re-layouts  7.53 us
    pallas_call x1, Pallas kernels, body(): pl.pallas_call(last_kernel, name='last', out_shape=jax.ShapeDtypeStruct((...  4.77 us

profile of v1, /device:TPU:1, one launch (start us, length us, event | category | flops | bytes accessed | tf_op | source)
XLA Modules:
  0.0 75.1 jit_solution(17384734131286000568)
XLA Ops:
  0.0 0.0 copy-start.7
  0.0 0.0 copy-start.8
  0.0 0.0 copy-start.9
  0.0 0.9 %copy.13 = f32[2,16,4,8]{3,2,1,0:T(4,128)S(1)} copy(f32[2,16,4,8]{1,3,2,0:T(8,128)} %param.13) | data formatting | bytes 8192 | tf_op args[1]
  0.9 0.0 copy-done.7
  0.9 0.0 copy-done.8
  0.9 0.0 copy-done.9
  0.9 0.0 copy-start.1
  0.9 1.2 %copy-done.1 = f32[32,1,32,256]{3,2,1,0:T(8,128)S(1)} copy-done((f32[32,1,32,256]{3,2,1,0:T(8,128)S(1)}, f32[32,1,32,256]{3,2,1,0:T(8,128)}, u32[]{:S(2)}) %copy-start.1) | copy-done | bytes 1048600
  2.2 0.0 copy-start.2
  2.2 1.0 %copy-done.2 = bf16[2,2,256,256]{3,2,1,0:T(8,128)(2,1)S(1)} copy-done((bf16[2,2,256,256]{3,2,1,0:T(8,128)(2,1)S(1)}, bf16[2,2,256,256]{3,2,1,0:T(8,128)(2,1)}, u32[]{:S(2)}) %copy-start.2) | copy-done | bytes 524312
  3.2 0.0 copy-start.3
  3.2 0.9 %copy-done.3 = f32[4,4,16,256]{3,2,1,0:T(8,128)S(1)} copy-done((f32[4,4,16,256]{3,2,1,0:T(8,128)S(1)}, f32[4,4,16,256]{3,2,1,0:T(8,128)}, u32[]{:S(2)}) %copy-start.3) | copy-done | bytes 262168
  4.1 0.0 copy-start.4
  4.1 0.9 %copy-done.4 = bf16[128,512]{1,0:T(8,128)(2,1)S(1)} copy-done((bf16[128,512]{1,0:T(8,128)(2,1)S(1)}, bf16[128,512]{1,0:T(8,128)(2,1)}, u32[]{:S(2)}) %copy-start.4) | copy-done | bytes 131096
  5.1 0.0 copy-start.6
  5.1 0.9 %copy-done.6 = f32[16,16,32]{2,1,0:T(8,128)S(1)} copy-done((f32[16,16,32]{2,1,0:T(8,128)S(1)}, f32[16,16,32]{2,1,0:T(8,128)}, u32[]{:S(2)}) %copy-start.6) | copy-done | bytes 32792
  6.0 62.8 %wide.1 = (f32[32,8,128]{2,1,0:T(8,128)S(1)}, f32[32,32,256]{2,1,0:T(8,128)S(1)}) custom-call(f32[32,32,256]{2,1,0:T(8,128)S(1)} %bitcast.5, f32[128,8]{1,0:T(8,128)S(1)} %bitcast.6, f32[32,27]{1,0:T(8,128)S(1)} %copy-done.7, f32[32,32]{1,0:T(8,128)S(1)} %copy-done.8, bf16[2,2,256,256]{3,2,1,0:T(8,128)(2,1)S(1)} %copy-done.2, ...), custom_call_target="tpu_custom_call" | custom-call | tf_op jit(solution)/shard_map/wide/pallas_call | solution.py:480
  68.7 0.0 copy-start
  68.7 1.0 %copy-done = f32[32,32,256]{2,1,0:T(8,128)} copy-done((f32[32,32,256]{2,1,0:T(8,128)}, f32[32,32,256]{2,1,0:T(8,128)S(1)}, u32[]{:S(2)}) %copy-start) | copy-done | bytes 1048600
  69.7 0.0 copy-start.5
  69.7 0.7 copy-done.5
  70.4 4.8 %last.1 = f32[32,32,256]{2,1,0:T(8,128)} custom-call(f32[32,8,128]{2,1,0:T(8,128)} %copy-done.5, f32[32,32,256]{2,1,0:T(8,128)} %copy-done, f32[32]{0:T(128)} %bias.1, f32[4,4,32,128]{3,2,1,0:T(8,128)} %constant.16.clone.tyi, bf16[2,256,512]{2,1,0:T(8,128)(2,1)} %constant.20.clone.txi), custom_call_target="tpu_custom_call" | custom-call | tf_op jit(solution)/shard_map/last/pallas_call | solution.py:518
Async XLA Ops:
  0.0 0.9 %copy-start.7 = (f32[32,27]{1,0:T(8,128)S(1)}, f32[32,27]{1,0:T(8,128)}, u32[]{:S(2)}) copy-start(f32[32,27]{1,0:T(8,128)} %depth_w.1) | copy-start | bytes 10372
  0.0 0.9 %copy-start.8 = (f32[32,32]{1,0:T(8,128)S(1)}, f32[32,32]{1,0:T(8,128)}, u32[]{:S(2)}) copy-start(f32[32,32]{1,0:T(8,128)} %point_w.1) | copy-start | bytes 12292
  0.0 0.9 %copy-start.9 = (bf16[64,128]{1,0:T(8,128)(2,1)S(1)}, bf16[64,128]{1,0:T(8,128)(2,1)}, u32[]{:S(2)}) copy-start(bf16[64,128]{1,0:T(8,128)(2,1)} %constant.17.clone.tz) | copy-start | bytes 49156
  0.9 1.2 %copy-start.1 = (f32[32,1,32,256]{3,2,1,0:T(8,128)S(1)}, f32[32,1,32,256]{3,2,1,0:T(8,128)}, u32[]{:S(2)}) copy-start(f32[32,1,32,256]{3,2,1,0:T(8,128)} %param.12) | copy-start | bytes 3145732
  2.2 1.0 %copy-start.2 = (bf16[2,2,256,256]{3,2,1,0:T(8,128)(2,1)S(1)}, bf16[2,2,256,256]{3,2,1,0:T(8,128)(2,1)}, u32[]{:S(2)}) copy-start(bf16[2,2,256,256]{3,2,1,0:T(8,128)(2,1)} %constant.14.clone.tx) | copy-start | bytes 1572868
  3.2 0.9 %copy-start.3 = (f32[4,4,16,256]{3,2,1,0:T(8,128)S(1)}, f32[4,4,16,256]{3,2,1,0:T(8,128)}, u32[]{:S(2)}) copy-start(f32[4,4,16,256]{3,2,1,0:T(8,128)} %constant.15.clone.ty) | copy-start | bytes 786436
  4.1 0.9 %copy-start.4 = (bf16[128,512]{1,0:T(8,128)(2,1)S(1)}, bf16[128,512]{1,0:T(8,128)(2,1)}, u32[]{:S(2)}) copy-start(bf16[128,512]{1,0:T(8,128)(2,1)} %constant.19.clone.te) | copy-start | bytes 393220
  5.1 0.9 %copy-start.6 = (f32[16,16,32]{2,1,0:T(8,128)S(1)}, f32[16,16,32]{2,1,0:T(8,128)}, u32[]{:S(2)}) copy-start(f32[16,16,32]{2,1,0:T(8,128)} %constant.18.clone.tzi) | copy-start | bytes 98308
  68.7 1.0 %copy-start = (f32[32,32,256]{2,1,0:T(8,128)}, f32[32,32,256]{2,1,0:T(8,128)S(1)}, u32[]{:S(2)}) copy-start(f32[32,32,256]{2,1,0:T(8,128)S(1)} %get-tuple-element.8.point) | copy-start | bytes 3145732
  69.7 0.7 copy-start.5

commit v2 on v1

--- a/solution.py
+++ b/solution.py
@@ -20,6 +20,7 @@
 ZC = 16
 W = 8
 YL = NY // GY
+VMEM_ALL = 67043328
 MESH = pl.DeviceIdType.MESH
 F32 = jnp.float32
 BF16 = jnp.bfloat16
@@ -64,18 +65,12 @@
     tables["tyi"] = np.repeat(mine.transpose(0, 1, 3, 2), 8, axis=3)
     angle = 2 * np.pi * (kept(MZ, NZ)[:, None] * np.arange(NZ)[None, :] % NZ) / NZ
     high, low = halves(np.concatenate([np.cos(angle), np.sin(angle)], axis=0))
-    tables["tz"] = np.concatenate([high, low], axis=0)
+    both = np.concatenate([high, low], axis=0).reshape(64, ZC, 2, 4)
+    tables["tz"] = both.transpose(2, 0, 1, 3).reshape(128, 64)
     scale = (NX * NY * NZ) ** -0.5 * (2.0 * MX * MY * MZ) ** -0.5
     both = np.concatenate([np.cos(angle), np.sin(angle)], axis=0).T * scale
-    high, low = halves(both)
-    tables["tzi"] = np.concatenate(
-        [high.reshape(ZC, W, 32), low.reshape(ZC, W, 32)], axis=1
-    ).astype(np.float32)
-    row = np.arange(128)[:, None]
-    col = np.arange(512)[None, :]
-    tables["te"] = (
-        (row // 32 == col // 128) & (row % 32 // 8 == col % 64 // 16) & (row % 8 == col % 8)
-    ).astype(ml_dtypes.bfloat16)
+    both = both.reshape(ZC, 2, 4, 32).transpose(1, 0, 2, 3).reshape(128, 32)
+    tables["tzi"] = np.concatenate(halves(both), axis=0)
     weight = np.where(np.arange(MX) == 0, 1.0, 2.0)[:, None]
     angle = 2 * np.pi * (np.arange(MX)[:, None] * np.arange(NX)[None, :] % NX) / NX
     cos = (weight * np.cos(angle)).reshape(4, 8, NX)
@@ -118,11 +113,12 @@
 
 
 def wide_kernel(
-    field3, filt, depth_w, point_w, tx, ty, tz, tzi, te,
+    field3, filt_in, depth_in, point_in, tx_in, ty_in, tz_in, tzi_in,
     tiles_out, point_out,
-    fv, pad, edge, hrow, xh, xl, yout, send1, recv1, tmp, send2, agbuf, gains,
-    fscr, ftile, fbuf, tmp3, depth, pacc,
-    ld_sem, s1, r1, sf, rf, sh, rh, sz, rz, s2, r2, s3, r3, so,
+    fv, filt, depth_w, point_w, tx, ty, tz, tzi,
+    pad, edge, hrow, xh, xl, yout, send1, recv1, tmp, send2, recv2, gains,
+    send4, recv4, tmp4, tmp3, depth, pacc,
+    ld_sem, s1, r1, sh, rh, sz, rz, s2, r2, s4, r4, s3, r3, so,
 ):
     gz = lax.axis_index("gz")
     gy = lax.axis_index("gy")
@@ -160,25 +156,30 @@
             signal(halo_peer(dz, dy))
     lax.fori_loop(1, 32, greet_plane, 0)
 
-    load = pltpu.make_async_copy(field3, fv, ld_sem.at[0])
-    load.start()
-    load_mid = pltpu.make_async_copy(field3, pad.at[1, :, 8:40, :], ld_sem.at[1])
-    load_mid.start()
-
-    fscr[...] = jnp.zeros_like(fscr)
-    fscr[:, 0:8] = filt[...]
-    tile = jnp.zeros((8, 128), F32)
-    for b in range(4):
-        for ky in range(4):
-            piece = fscr[pl.ds(b * 32 + ky, 8, stride=4), :]
-            shift = b * 32 + ky * 8
-            tile = tile + (piece if shift == 0 else pltpu.roll(piece, shift, 1))
-    ftile[...] = tile
-
-    load.wait()
+    loads = [
+        pltpu.make_async_copy(src, dst, ld_sem.at[k])
+        for k, (src, dst) in enumerate(
+            [
+                (field3, fv),
+                (tx_in, tx),
+                (ty_in.at[gy], ty),
+                (field3, pad.at[1, :, 8:40, :]),
+                (filt_in, filt),
+                (depth_in, depth_w),
+                (point_in, point_w),
+                (tz_in, tz),
+                (tzi_in, tzi),
+            ]
+        )
+    ]
+    for load in loads:
+        load.start()
+    loads[0].wait()
     for side, row in ((0, YL - 1), (1, 0)):
         edge[side] = fv[:, row, :]
 
+    loads[1].wait()
+    loads[2].wait()
     for p in range(2):
         total = None
         for ml in range(2):
@@ -196,7 +197,7 @@
     same = iota((MY, 8, 256), 1) == iota((MY, 8, 256), 2) // YL
 
     def spread(which):
-        base = ty[gy, which]
+        base = ty[which]
         wide = jnp.where(same, jnp.broadcast_to(base[:, None, :], (MY, 8, 256)), 0.0)
         return wide.reshape(128, 256).astype(BF16)
 
@@ -234,15 +235,6 @@
     own1 = pltpu.make_async_copy(send1.at[me], recv1.at[me], r1)
     own1.start()
 
-    def copyf(i):
-        return pltpu.make_async_remote_copy(
-            ftile, fbuf.at[zc], sf, rf, device_id=(ring_peer(i), gy), device_id_type=MESH
-        )
-
-    def startf(i, carry):
-        copyf(i).start()
-        return carry
-
     def copy_row(dz, side):
         dy = 1 if side == 0 else -1
         slot = (1 - dz) * 2 + side
@@ -264,29 +256,36 @@
     for dz in (-1, 1):
         for side in range(2):
             copy_row(dz, side).start()
-    lax.fori_loop(1, ZC, startf, 0)
-    own_f = pltpu.make_async_copy(ftile, fbuf.at[zc], rf)
-    own_f.start()
+    for load in loads[4:]:
+        load.wait()
+    gains[...] = jnp.zeros_like(gains)
+    for part in range(2):
+        for ky in range(4):
+            for r in range(2):
+                row = part * 64 + ky * 16 + r * 8
+                gains[row : row + 8, 0:16] = filt[part * 32 + ky * 8 : part * 32 + ky * 8 + 8, :]
 
     def put_rows(plane, slot):
         pad[plane, :, 7, :] = hrow[slot]
         pad[plane, :, 40, :] = hrow[slot + 1]
 
     def conv(plane, first):
-        def channel(c, carry):
-            sums = [None, None, None]
-            for b in range(3):
-                window = pad[plane, c, 7 + b : 39 + b, :]
-                for e in range(3):
-                    term = depth_w[c, plane * 9 + b * 3 + e] * window
-                    sums[e] = term if sums[e] is None else sums[e] + term
-            value = sums[1] + pltpu.roll(sums[0], 1, 1) + pltpu.roll(sums[2], NX - 1, 1)
-            depth[c] = value if first else depth[c] + value
+        def channels(step, carry):
+            for k in range(4):
+                c = step * 4 + k
+                sums = [None, None, None]
+                for b in range(3):
+                    window = pad[plane, c, 7 + b : 39 + b, :]
+                    for e in range(3):
+                        term = depth_w[c, plane * 9 + b * 3 + e] * window
+                        sums[e] = term if sums[e] is None else sums[e] + term
+                value = sums[1] + pltpu.roll(sums[0], 1, 1) + pltpu.roll(sums[2], NX - 1, 1)
+                depth[c] = value if first else depth[c] + value
             return carry
 
-        lax.fori_loop(0, C, channel, 0)
-
-    load_mid.wait()
+        lax.fori_loop(0, C // 4, channels, 0)
+
+    loads[3].wait()
 
     def wait_rows(index, count):
         part = hrow.at[0:count]
@@ -299,40 +298,30 @@
     pltpu.make_async_copy(recv1, recv1, r1).wait()
     for k in range(W):
         tmp[k * 8 : (k + 1) * 8, :] = (recv1[k] + recv1[8 + k]) + (recv1[16 + k] + recv1[24 + k])
+    lower = iota((8, 128), 1) < 64
     for s in range(8):
-        send2[:, s * 128 : (s + 1) * 128] = tmp[pl.ds(s, 8, stride=8), :]
+        part = tmp[pl.ds(s, 8, stride=8), :]
+        turned = pltpu.roll(part, 64, 1)
+        send2[2 * s] = jnp.where(lower[0:4], part[0:4], turned[4:8])
+        send2[2 * s + 1] = jnp.where(lower[0:4], turned[0:4], part[4:8])
 
     def far_first(k):
         return 8 + (k + 1) // 2 * (2 * (k % 2) - 1)
 
-    def copy2(k):
+    def copy2(k, src, dst, ssem, rsem):
+        i = far_first(k)
         return pltpu.make_async_remote_copy(
-            send2, agbuf.at[zc], s2, r2, device_id=(ring_peer(far_first(k)), gy), device_id_type=MESH
+            src.at[(zc + i) % ZC], dst.at[zc], ssem, rsem,
+            device_id=(ring_peer(i), gy), device_id_type=MESH,
         )
 
     def start2(k, carry):
-        copy2(k).start()
+        copy2(k, send2, recv2, s2, r2).start()
         return carry
 
     lax.fori_loop(0, ZC - 1, start2, 0)
-    own2 = pltpu.make_async_copy(send2, agbuf.at[zc], r2)
+    own2 = pltpu.make_async_copy(send2.at[zc], recv2.at[zc], r2)
     own2.start()
-
-    pltpu.make_async_copy(fbuf, fbuf, rf).wait()
-    raw = fbuf[...].reshape(128, 128)
-    high = raw.astype(BF16)
-    rest = raw - high.astype(F32)
-    mid = rest.astype(BF16)
-    low = (rest - mid.astype(F32)).astype(BF16)
-    wide = dot(high, te[...]) + dot(mid, te[...]) + dot(low, te[...])
-    lower = iota((8, 128), 1) < 64
-    for part in range(2):
-        for h in range(2):
-            lanes = slice((part * 2 + h) * 128, (part * 2 + h + 1) * 128)
-            for s in range(8):
-                gains[part, h * 8 : (h + 1) * 8, s * 128 : (s + 1) * 128] = jnp.where(
-                    lower, wide[s * 16 : s * 16 + 8, lanes], wide[s * 16 + 8 : s * 16 + 16, lanes]
-                )
 
     wait_rows(1, 4)
     near = jnp.where(core == 0, 2, 0)
@@ -341,23 +330,44 @@
     put_rows(near, near * 2)
     conv(near, False)
 
-    pltpu.make_async_copy(agbuf, agbuf, r2).wait()
-    a_high, a_low = split(agbuf[...].reshape(NZ, 1024))
+    pltpu.make_async_copy(recv2, recv2, r2).wait()
+    a_high, a_low = split(recv2[...].reshape(64, 128))
     both = dot(tz[...], a_high) + dot(tz[...], a_low)
+    both = both[0:64] + pltpu.roll(both[64:128], 64, 1)
     modes = both[0:16] + both[32:48] + swapped(both[16:32] + both[48:64])
-    filtered = modes * gains[0] - swapped(modes) * gains[1]
+    turned = jnp.transpose(gains[...])[0:16, :]
+    filtered = modes * turned - swapped(modes) * pltpu.roll(turned, 64, 1)
     stacked = jnp.concatenate([filtered, -swapped(filtered)], axis=0)
     f_high, f_low = split(stacked)
-    table = tzi[zc].astype(BF16)
-    both = dot(table, f_high) + dot(table, f_low)
-    back = both[0:8] + both[8:16]
-    for s in range(8):
-        tmp3[pl.ds(s, 8, stride=8), :] = back[:, s * 128 : (s + 1) * 128]
+    both = dot(tzi[...], f_high) + dot(tzi[...], f_low)
+    both = both[0:128] + both[128:256]
+    back = jnp.where(iota((64, 128), 1) < 64, both[0:64], pltpu.roll(both[64:128], 64, 1))
+    send4[...] = back.reshape(ZC, 4, 128)
+
+    def start4(k, carry):
+        copy2(k, send4, recv4, s4, r4).start()
+        return carry
+
+    lax.fori_loop(0, ZC - 1, start4, 0)
+    own4 = pltpu.make_async_copy(send4.at[zc], recv4.at[zc], r4)
+    own4.start()
+
+    pltpu.make_async_copy(field3, pad.at[far, :, 8:40, :], rz.at[far]).wait()
+    put_rows(far, far * 2)
+    conv(far, False)
+
+    pltpu.make_async_copy(recv4, recv4, r4).wait()
+    tmp4[...] = recv4[...].reshape(64, 128)
+    for i in range(4):
+        even = tmp4[pl.ds(i, 8, stride=8), :]
+        odd = tmp4[pl.ds(4 + i, 8, stride=8), :]
+        tmp3[i] = jnp.where(lower, even, pltpu.roll(odd, 64, 1))
+        tmp3[4 + i] = jnp.where(lower, pltpu.roll(even, 64, 1), odd)
 
     def copy3(i):
         target, t = plane_peer(i)
         return pltpu.make_async_remote_copy(
-            tmp3.at[pl.ds(pl.multiple_of(t % W * 8, 8), 8), :], tiles_out.at[w * 4 + gy], s3, r3,
+            tmp3.at[t % W], tiles_out.at[w * 4 + gy], s3, r3,
             device_id=target, device_id_type=MESH,
         )
 
@@ -367,13 +377,9 @@
 
     lax.fori_loop(1, 32, start3, 0)
     own3 = pltpu.make_async_copy(
-        tmp3.at[pl.ds(pl.multiple_of(w * 8, 8), 8), :], tiles_out.at[w * 4 + gy], r3
+        tmp3.at[w], tiles_out.at[w * 4 + gy], r3
     )
     own3.start()
-
-    pltpu.make_async_copy(field3, pad.at[far, :, 8:40, :], rz.at[far]).wait()
-    put_rows(far, far * 2)
-    conv(far, False)
 
     grow = (iota((256, C), 0) // 8 == iota((256, C), 1)).astype(F32).astype(BF16)
     grow_t = (iota((C, 256), 1) // 8 == iota((C, 256), 0)).astype(F32).astype(BF16)
@@ -398,16 +404,12 @@
         return carry
 
     def done2(k, carry):
-        copy2(k).wait_send()
-        return carry
-
-    def donef(i, carry):
-        copyf(i).wait_send()
+        copy2(k, send2, recv2, s2, r2).wait_send()
+        copy2(k, send4, recv4, s4, r4).wait_send()
         return carry
 
     lax.fori_loop(1, 32, done1, 0)
     lax.fori_loop(0, ZC - 1, done2, 0)
-    lax.fori_loop(1, ZC, donef, 0)
     for dz in (-1, 0, 1):
         for side in range(2):
             copy_row(dz, side).wait_send()
@@ -472,11 +474,11 @@
 
 def body(field, spectral_filter, depth_weight, point_weight, bias_vector):
     field3 = field.reshape(C, YL, NX)
-    filt = spectral_filter.reshape(128, 8)
+    filt = spectral_filter.transpose(0, 2, 3, 1).reshape(64, 16)
     const = {name: jnp.asarray(value) for name, value in TABLES.items()}
     vmem = pl.BlockSpec(memory_space=pltpu.VMEM)
     smem = pl.BlockSpec(memory_space=pltpu.SMEM)
-    hbm = pl.BlockSpec(memory_space=pl.ANY)
+    hbm = pl.BlockSpec(memory_space=pltpu.HBM)
     tiles, point = pl.pallas_call(
         wide_kernel,
         name="wide",
@@ -484,10 +486,17 @@
             jax.ShapeDtypeStruct((32, 8, 128), F32),
             jax.ShapeDtypeStruct((C, YL, NX), F32),
         ),
-        in_specs=[hbm, vmem, smem, vmem, vmem, vmem, vmem, vmem, vmem],
+        in_specs=[hbm] * 8,
         out_specs=(hbm, hbm),
         scratch_shapes=[
             VMEM((C, YL, NX), F32),
+            VMEM((64, 16), F32),
+            pltpu.SMEM((C, 27), F32),
+            VMEM((C, C), F32),
+            VMEM((2, 2, 256, 256), BF16),
+            VMEM((4, MY, 256), F32),
+            VMEM((128, 64), BF16),
+            VMEM((256, 32), BF16),
             VMEM((3, C, 48, NX), F32),
             VMEM((2, C, NX), F32),
             VMEM((6, C, NX), F32),
@@ -497,23 +506,23 @@
             VMEM((32, 8, 128), F32),
             VMEM((32, 8, 128), F32),
             VMEM((64, 128), F32),
-            VMEM((8, 1024), F32),
-            VMEM((ZC, 8, 1024), F32),
-            VMEM((2, 16, 1024), F32),
+            VMEM((ZC, 4, 128), F32),
+            VMEM((ZC, 4, 128), F32),
             VMEM((128, 128), F32),
-            VMEM((8, 128), F32),
-            VMEM((ZC, 8, 128), F32),
+            VMEM((ZC, 4, 128), F32),
+            VMEM((ZC, 4, 128), F32),
             VMEM((64, 128), F32),
+            VMEM((W, 8, 128), F32),
             VMEM((C, YL, NX), F32),
             VMEM((C, YL, NX), F32),
-            DMA((2,)), DMA, DMA, DMA, DMA, DMA, DMA((2,)), DMA, DMA((3,)), DMA, DMA, DMA, DMA, DMA,
+            DMA((9,)), DMA, DMA, DMA, DMA((2,)), DMA, DMA((3,)), DMA, DMA, DMA, DMA, DMA, DMA, DMA,
         ],
         compiler_params=pltpu.CompilerParams(
-            collective_id=0, has_side_effects=True, vmem_limit_bytes=40 * 1024 * 1024
+            collective_id=0, has_side_effects=True, vmem_limit_bytes=VMEM_ALL
         ),
     )(
         field3, filt, depth_weight, point_weight,
-        const["tx"], const["ty"], const["tz"], const["tzi"], const["te"],
+        const["tx"], const["ty"], const["tz"], const["tzi"],
     )
     out = pl.pallas_call(
         last_kernel,
@@ -529,7 +538,7 @@
         ],
         out_specs=pl.BlockSpec((8, YL, NX), lambda i: (i, 0, 0)),
         scratch_shapes=[VMEM((512, 256), BF16), VMEM((512, 256), BF16)],
-        compiler_params=pltpu.CompilerParams(dimension_semantics=("arbitrary",)),
+        compiler_params=pltpu.CompilerParams(dimension_semantics=("arbitrary",), vmem_limit_bytes=VMEM_ALL),
     )(tiles, point, bias_vector, const["tyi"], const["txi"])
     return out.reshape(C, 1, YL, NX)
 

time: 75.5 us -> 54.7 us (0.72)
  Pallas kernels: 67.5 us -> 54.5 us
  local copies, waits for them, and re-layouts: 7.53 us -> 0 us
    pallas_call x1, Pallas kernels: 62.8 us -> 49.7 us  [body(): pl.pallas_call(wide_kernel, name='wide', out_shape=(jax.ShapeDtypeStruct(...]
    unnamed x21 -> x0, local copies, waits for them, and re-layouts: 7.53 us -> none
where the time goes in v2:
time: 54.7 us; the launch traced here: 54.5 us
  Pallas kernels  54.5 us (100%)
    pallas_call x1, Pallas kernels, body(): pl.pallas_call(wide_kernel, name='wide', out_shape=(jax.ShapeDtypeStruct(...  49.7 us
    pallas_call x1, Pallas kernels, body(): pl.pallas_call(last_kernel, name='last', out_shape=jax.ShapeDtypeStruct((...  4.79 us

profile of v2, /device:TPU:1, one launch (start us, length us, event | category | flops | bytes accessed | tf_op | source)
XLA Modules:
  0.0 54.5 jit_solution(14702411167604971616)
XLA Ops:
  0.0 49.7 %wide.1 = (f32[32,8,128]{2,1,0:T(8,128)}, f32[32,32,256]{2,1,0:T(8,128)}) custom-call(f32[32,32,256]{2,1,0:T(8,128)} %bitcast.7, f32[64,16]{1,0:T(8,128)} %bitcast.8, f32[32,27]{1,0:T(8,128)} %depth_in.1, f32[32,32]{1,0:T(8,128)} %point_in.1, bf16[2,2,256,256]{3,2,1,0:T(8,128)(2,1)} %constant.12.clone.tx_in, f32[4,4,16,256]{3,2,1,0:T(8,128)} %constant.13.clone.ty_in, ...), custom_call_target="tpu_custom_call" | custom-call | tf_op jit(solution)/shard_map/wide/pallas_call | solution.py:482
  49.7 4.8 %last.1 = f32[32,32,256]{2,1,0:T(8,128)} custom-call(f32[32,8,128]{2,1,0:T(8,128)} %get-tuple-element.7.tiles, f32[32,32,256]{2,1,0:T(8,128)} %get-tuple-element.8.point, f32[32]{0:T(128)} %bias.1, f32[4,4,32,128]{3,2,1,0:T(8,128)} %constant.14.clone.tyi, bf16[2,256,512]{2,1,0:T(8,128)(2,1)} %constant.17.clone.txi), custom_call_target="tpu_custom_call" | custom-call | tf_op jit(solution)/shard_map/last/pallas_call | solution.py:527

commit v3 on v2

--- a/solution.py
+++ b/solution.py
@@ -65,11 +65,9 @@
     tables["tyi"] = np.repeat(mine.transpose(0, 1, 3, 2), 8, axis=3)
     angle = 2 * np.pi * (kept(MZ, NZ)[:, None] * np.arange(NZ)[None, :] % NZ) / NZ
     high, low = halves(np.concatenate([np.cos(angle), np.sin(angle)], axis=0))
-    both = np.concatenate([high, low], axis=0).reshape(64, ZC, 2, 4)
-    tables["tz"] = both.transpose(2, 0, 1, 3).reshape(128, 64)
+    tables["tz"] = np.concatenate([high, low], axis=0)
     scale = (NX * NY * NZ) ** -0.5 * (2.0 * MX * MY * MZ) ** -0.5
     both = np.concatenate([np.cos(angle), np.sin(angle)], axis=0).T * scale
-    both = both.reshape(ZC, 2, 4, 32).transpose(1, 0, 2, 3).reshape(128, 32)
     tables["tzi"] = np.concatenate(halves(both), axis=0)
     weight = np.where(np.arange(MX) == 0, 1.0, 2.0)[:, None]
     angle = 2 * np.pi * (np.arange(MX)[:, None] * np.arange(NX)[None, :] % NX) / NX
@@ -115,10 +113,10 @@
 def wide_kernel(
     field3, filt_in, depth_in, point_in, tx_in, ty_in, tz_in, tzi_in,
     tiles_out, point_out,
-    fv, filt, depth_w, point_w, tx, ty, tz, tzi,
+    fv, filt, filt2, depth_w, point_w, tx, ty, tz, tzi,
     pad, edge, hrow, xh, xl, yout, send1, recv1, tmp, send2, recv2, gains,
-    send4, recv4, tmp4, tmp3, depth, pacc,
-    ld_sem, s1, r1, sh, rh, sz, rz, s2, r2, s4, r4, s3, r3, so,
+    send4, recv4, tmp3, depth, pacc,
+    ld_sem, s1, r1, sh, rh, sz, rz, s2, r2, s4, r4, s3, r3, so, sf, rf, tokens,
 ):
     gz = lax.axis_index("gz")
     gy = lax.axis_index("gy")
@@ -142,19 +140,9 @@
     def signal(target):
         pl.semaphore_signal(barrier, inc=1, device_id=target, device_id_type=MESH)
 
-    def greet_ring(i, carry):
-        signal((ring_peer(i), gy))
-        return carry
-
     def greet_plane(i, carry):
         signal(plane_peer(i)[0])
         return carry
-
-    lax.fori_loop(1, ZC, greet_ring, 0)
-    for dz in (-1, 1):
-        for dy in (-1, 0, 1):
-            signal(halo_peer(dz, dy))
-    lax.fori_loop(1, 32, greet_plane, 0)
 
     loads = [
         pltpu.make_async_copy(src, dst, ld_sem.at[k])
@@ -172,9 +160,17 @@
             ]
         )
     ]
-    for load in loads:
+    for load in loads[:3]:
         load.start()
+    for i in (2, ZC - 2, 1, ZC - 1):
+        signal((ring_peer(i), gy))
+    for dz in (-1, 1):
+        for dy in (-1, 0, 1):
+            signal(halo_peer(dz, dy))
+    lax.fori_loop(1, 32, greet_plane, 0)
     loads[0].wait()
+    for load in loads[3:]:
+        load.start()
     for side, row in ((0, YL - 1), (1, 0)):
         edge[side] = fv[:, row, :]
 
@@ -219,7 +215,7 @@
                     out = jnp.where(block == ky, moved(quad[ky], ky - kxb), out)
                 send1[q * 8 + p * 4 + kxb] = out
 
-    pl.semaphore_wait(barrier, 15 + 6 + 31)
+    pl.semaphore_wait(barrier, 4 + 6 + 31)
 
     def copy1(i):
         target, t = plane_peer(i)
@@ -249,6 +245,13 @@
             device_id=halo_peer(dz, 0), device_id_type=MESH,
         )
 
+    def send_tokens(which, reach):
+        for i in (reach, ZC - reach):
+            pl.semaphore_signal(
+                tokens.at[which], inc=1, device_id=(ring_peer(i), gy), device_id_type=MESH
+            )
+
+    send_tokens(0, 2)
     for side in range(2):
         copy_row(0, side).start()
     for dz in (-1, 1):
@@ -256,14 +259,17 @@
     for dz in (-1, 1):
         for side in range(2):
             copy_row(dz, side).start()
+    def put_gains(source, pair):
+        for part in range(2):
+            for ky in range(4):
+                for r in range(2):
+                    row = pl.multiple_of(pair * 64 + ky * 16 + r * 8, 8)
+                    gains[part, pl.ds(row, 8), 0:16] = source[part * 32 + ky * 8 : part * 32 + ky * 8 + 8, :]
+
     for load in loads[4:]:
         load.wait()
     gains[...] = jnp.zeros_like(gains)
-    for part in range(2):
-        for ky in range(4):
-            for r in range(2):
-                row = part * 64 + ky * 16 + r * 8
-                gains[row : row + 8, 0:16] = filt[part * 32 + ky * 8 : part * 32 + ky * 8 + 8, :]
+    put_gains(filt, zc // 8)
 
     def put_rows(plane, slot):
         pad[plane, :, 7, :] = hrow[slot]
@@ -292,6 +298,8 @@
         pltpu.make_async_copy(part, part, rh.at[index]).wait()
 
     wait_rows(0, 2)
+    pl.semaphore_wait(tokens.at[0], 2)
+    send_tokens(1, 4)
     put_rows(1, 2)
     conv(1, True)
 
@@ -299,28 +307,33 @@
     for k in range(W):
         tmp[k * 8 : (k + 1) * 8, :] = (recv1[k] + recv1[8 + k]) + (recv1[16 + k] + recv1[24 + k])
     lower = iota((8, 128), 1) < 64
-    for s in range(8):
-        part = tmp[pl.ds(s, 8, stride=8), :]
-        turned = pltpu.roll(part, 64, 1)
-        send2[2 * s] = jnp.where(lower[0:4], part[0:4], turned[4:8])
-        send2[2 * s + 1] = jnp.where(lower[0:4], turned[0:4], part[4:8])
-
-    def far_first(k):
-        return 8 + (k + 1) // 2 * (2 * (k % 2) - 1)
-
-    def copy2(k, src, dst, ssem, rsem):
-        i = far_first(k)
+    for k in range(8):
+        one = tmp[pl.ds(k // 2, 8, stride=8), :]
+        two = tmp[pl.ds(k // 2 + 4, 8, stride=8), :]
+        if k % 2 == 0:
+            send2[k] = jnp.where(lower, one, pltpu.roll(two, 64, 1))
+        else:
+            send2[k] = jnp.where(lower, pltpu.roll(one, 64, 1), two)
+
+    pl.semaphore_wait(tokens.at[1], 2)
+
+    def copy2(k):
+        i = 8 + (k + 1) // 2 * (2 * (k % 2) - 1)
         return pltpu.make_async_remote_copy(
-            src.at[(zc + i) % ZC], dst.at[zc], ssem, rsem,
+            send2.at[(zc + i) % 8], recv2.at[zc], s2, r2,
             device_id=(ring_peer(i), gy), device_id_type=MESH,
         )
 
     def start2(k, carry):
-        copy2(k, send2, recv2, s2, r2).start()
+        copy2(k).start()
         return carry
 
+    copyf = pltpu.make_async_remote_copy(
+        filt_in, filt2, sf, rf, device_id=(ring_peer(8), gy), device_id_type=MESH
+    )
+    copyf.start()
     lax.fori_loop(0, ZC - 1, start2, 0)
-    own2 = pltpu.make_async_copy(send2.at[zc], recv2.at[zc], r2)
+    own2 = pltpu.make_async_copy(send2.at[zc % 8], recv2.at[zc], r2)
     own2.start()
 
     wait_rows(1, 4)
@@ -330,26 +343,32 @@
     put_rows(near, near * 2)
     conv(near, False)
 
+    copyf.wait_recv()
+    put_gains(filt2, 1 - zc // 8)
+    gain_re = jnp.transpose(gains[0])[0:16, :]
+    gain_im = jnp.transpose(gains[1])[0:16, :]
     pltpu.make_async_copy(recv2, recv2, r2).wait()
-    a_high, a_low = split(recv2[...].reshape(64, 128))
+    a_high, a_low = split(recv2[...].reshape(NZ, 128))
     both = dot(tz[...], a_high) + dot(tz[...], a_low)
-    both = both[0:64] + pltpu.roll(both[64:128], 64, 1)
     modes = both[0:16] + both[32:48] + swapped(both[16:32] + both[48:64])
-    turned = jnp.transpose(gains[...])[0:16, :]
-    filtered = modes * turned - swapped(modes) * pltpu.roll(turned, 64, 1)
+    filtered = modes * gain_re - swapped(modes) * gain_im
     stacked = jnp.concatenate([filtered, -swapped(filtered)], axis=0)
     f_high, f_low = split(stacked)
     both = dot(tzi[...], f_high) + dot(tzi[...], f_low)
-    both = both[0:128] + both[128:256]
-    back = jnp.where(iota((64, 128), 1) < 64, both[0:64], pltpu.roll(both[64:128], 64, 1))
-    send4[...] = back.reshape(ZC, 4, 128)
-
-    def start4(k, carry):
-        copy2(k, send4, recv4, s4, r4).start()
-        return carry
-
-    lax.fori_loop(0, ZC - 1, start4, 0)
-    own4 = pltpu.make_async_copy(send4.at[zc], recv4.at[zc], r4)
+    send4[...] = (both[0:128] + both[128:256]).reshape(ZC, 8, 128)
+
+    def copy4(i):
+        return pltpu.make_async_remote_copy(
+            send4.at[(zc + i) % ZC], recv4.at[pl.ds(pl.multiple_of(zc % 8 * 8, 8), 8), :], s4, r4,
+            device_id=(ring_peer(i), gy), device_id_type=MESH,
+        )
+
+    nearer = (ZC - 4, 3, ZC - 3, 2, ZC - 2, 1, ZC - 1)
+    for i in nearer:
+        copy4(i).start()
+    own4 = pltpu.make_async_copy(
+        send4.at[zc], recv4.at[pl.ds(pl.multiple_of(zc % 8 * 8, 8), 8), :], r4
+    )
     own4.start()
 
     pltpu.make_async_copy(field3, pad.at[far, :, 8:40, :], rz.at[far]).wait()
@@ -357,12 +376,11 @@
     conv(far, False)
 
     pltpu.make_async_copy(recv4, recv4, r4).wait()
-    tmp4[...] = recv4[...].reshape(64, 128)
-    for i in range(4):
-        even = tmp4[pl.ds(i, 8, stride=8), :]
-        odd = tmp4[pl.ds(4 + i, 8, stride=8), :]
-        tmp3[i] = jnp.where(lower, even, pltpu.roll(odd, 64, 1))
-        tmp3[4 + i] = jnp.where(lower, pltpu.roll(even, 64, 1), odd)
+    for k in range(W):
+        even = recv4[pl.ds(k, 4, stride=16), :]
+        odd = recv4[pl.ds(8 + k, 4, stride=16), :]
+        tmp3[k, 0:4] = jnp.where(lower[0:4], even, pltpu.roll(odd, 64, 1))
+        tmp3[k, 4:8] = jnp.where(lower[0:4], pltpu.roll(even, 64, 1), odd)
 
     def copy3(i):
         target, t = plane_peer(i)
@@ -404,12 +422,14 @@
         return carry
 
     def done2(k, carry):
-        copy2(k, send2, recv2, s2, r2).wait_send()
-        copy2(k, send4, recv4, s4, r4).wait_send()
+        copy2(k).wait_send()
         return carry
 
     lax.fori_loop(1, 32, done1, 0)
     lax.fori_loop(0, ZC - 1, done2, 0)
+    for i in nearer:
+        copy4(i).wait_send()
+    copyf.wait_send()
     for dz in (-1, 0, 1):
         for side in range(2):
             copy_row(dz, side).wait_send()
@@ -491,11 +511,12 @@
         scratch_shapes=[
             VMEM((C, YL, NX), F32),
             VMEM((64, 16), F32),
+            VMEM((64, 16), F32),
             pltpu.SMEM((C, 27), F32),
             VMEM((C, C), F32),
             VMEM((2, 2, 256, 256), BF16),
             VMEM((4, MY, 256), F32),
-            VMEM((128, 64), BF16),
+            VMEM((64, 128), BF16),
             VMEM((256, 32), BF16),
             VMEM((3, C, 48, NX), F32),
             VMEM((2, C, NX), F32),
@@ -506,16 +527,16 @@
             VMEM((32, 8, 128), F32),
             VMEM((32, 8, 128), F32),
             VMEM((64, 128), F32),
-            VMEM((ZC, 4, 128), F32),
-            VMEM((ZC, 4, 128), F32),
-            VMEM((128, 128), F32),
-            VMEM((ZC, 4, 128), F32),
-            VMEM((ZC, 4, 128), F32),
+            VMEM((8, 8, 128), F32),
+            VMEM((ZC, 8, 128), F32),
+            VMEM((2, 128, 128), F32),
+            VMEM((ZC, 8, 128), F32),
             VMEM((64, 128), F32),
             VMEM((W, 8, 128), F32),
             VMEM((C, YL, NX), F32),
             VMEM((C, YL, NX), F32),
-            DMA((9,)), DMA, DMA, DMA, DMA((2,)), DMA, DMA((3,)), DMA, DMA, DMA, DMA, DMA, DMA, DMA,
+            DMA((9,)), DMA, DMA, DMA, DMA((2,)), DMA, DMA((3,)), DMA, DMA, DMA, DMA, DMA, DMA, DMA, DMA, DMA,
+            pltpu.SemaphoreType.REGULAR((2,)),
         ],
         compiler_params=pltpu.CompilerParams(
             collective_id=0, has_side_effects=True, vmem_limit_bytes=VMEM_ALL

time: 54.7 us -> 53.4 us (0.976)
  Pallas kernels: 54.5 us -> 53.2 us
    pallas_call x1, Pallas kernels: 49.7 us -> 48.4 us  [body(): pl.pallas_call(wide_kernel, name='wide', out_shape=(jax.ShapeDtypeStruct(...]
where the time goes in v3:
time: 53.4 us; the launch traced here: 53.2 us
  Pallas kernels  53.2 us (100%)
    pallas_call x1, Pallas kernels, body(): pl.pallas_call(wide_kernel, name='wide', out_shape=(jax.ShapeDtypeStruct(...  48.4 us
    pallas_call x1, Pallas kernels, body(): pl.pallas_call(last_kernel, name='last', out_shape=jax.ShapeDtypeStruct((...  4.79 us

profile of v3, /device:TPU:1, one launch (start us, length us, event | category | flops | bytes accessed | tf_op | source)
XLA Modules:
  0.0 53.2 jit_solution(10176601486649179798)
XLA Ops:
  0.0 48.4 %wide.1 = (f32[32,8,128]{2,1,0:T(8,128)}, f32[32,32,256]{2,1,0:T(8,128)}) custom-call(f32[32,32,256]{2,1,0:T(8,128)} %bitcast.7, f32[64,16]{1,0:T(8,128)} %bitcast.8, f32[32,27]{1,0:T(8,128)} %depth_in.1, f32[32,32]{1,0:T(8,128)} %point_in.1, bf16[2,2,256,256]{3,2,1,0:T(8,128)(2,1)} %constant.12.clone.tx_in, f32[4,4,16,256]{3,2,1,0:T(8,128)} %constant.13.clone.ty_in, ...), custom_call_target="tpu_custom_call" | custom-call | tf_op jit(solution)/shard_map/wide/pallas_call | solution.py:502
  48.4 4.8 %last.1 = f32[32,32,256]{2,1,0:T(8,128)} custom-call(f32[32,8,128]{2,1,0:T(8,128)} %get-tuple-element.7.tiles, f32[32,32,256]{2,1,0:T(8,128)} %get-tuple-element.8.point, f32[32]{0:T(128)} %bias.1, f32[4,4,32,128]{3,2,1,0:T(8,128)} %constant.14.clone.tyi, bf16[2,256,512]{2,1,0:T(8,128)(2,1)} %constant.17.clone.txi), custom_call_target="tpu_custom_call" | custom-call | tf_op jit(solution)/shard_map/last/pallas_call | solution.py:548

commit v4 on v3

--- a/solution.py
+++ b/solution.py
@@ -21,6 +21,7 @@
 W = 8
 YL = NY // GY
 VMEM_ALL = 67043328
+CUTS = (8, 22)
 MESH = pl.DeviceIdType.MESH
 F32 = jnp.float32
 BF16 = jnp.bfloat16
@@ -239,11 +240,21 @@
             device_id=halo_peer(dz, dy), device_id_type=MESH,
         )
 
-    def copy_plane(dz):
+    to_near = 1 - 2 * core
+
+    def copy_plane(dz, chans):
         return pltpu.make_async_remote_copy(
-            field3, pad.at[1 - dz, :, 8:40, :], sz, rz.at[1 - dz],
+            field3.at[chans[0] : chans[1]], pad.at[1 - dz, chans[0] : chans[1], 8:40, :], sz, rz.at[1 - dz],
             device_id=halo_peer(dz, 0), device_id_type=MESH,
         )
+
+    parts = ((0, CUTS[0]), (CUTS[0], CUTS[1]), (CUTS[1], C))
+    crossing = jnp.logical_or(w == 0, w == W - 1)
+
+    def cross(part):
+        @pl.when(crossing)
+        def _():
+            copy_plane(-to_near, parts[part]).start()
 
     def send_tokens(which, reach):
         for i in (reach, ZC - reach):
@@ -254,8 +265,14 @@
     send_tokens(0, 2)
     for side in range(2):
         copy_row(0, side).start()
-    for dz in (-1, 1):
-        copy_plane(dz).start()
+    copy_plane(to_near, (0, C)).start()
+    cross(0)
+
+    @pl.when(jnp.logical_not(crossing))
+    def _():
+        for part in parts:
+            copy_plane(-to_near, part).start()
+
     for dz in (-1, 1):
         for side in range(2):
             copy_row(dz, side).start()
@@ -291,17 +308,8 @@
 
         lax.fori_loop(0, C // 4, channels, 0)
 
-    loads[3].wait()
-
-    def wait_rows(index, count):
-        part = hrow.at[0:count]
-        pltpu.make_async_copy(part, part, rh.at[index]).wait()
-
-    wait_rows(0, 2)
     pl.semaphore_wait(tokens.at[0], 2)
     send_tokens(1, 4)
-    put_rows(1, 2)
-    conv(1, True)
 
     pltpu.make_async_copy(recv1, recv1, r1).wait()
     for k in range(W):
@@ -335,6 +343,17 @@
     lax.fori_loop(0, ZC - 1, start2, 0)
     own2 = pltpu.make_async_copy(send2.at[zc % 8], recv2.at[zc], r2)
     own2.start()
+
+    cross(1)
+    loads[3].wait()
+
+    def wait_rows(index, count):
+        part = hrow.at[0:count]
+        pltpu.make_async_copy(part, part, rh.at[index]).wait()
+
+    wait_rows(0, 2)
+    put_rows(1, 2)
+    conv(1, True)
 
     wait_rows(1, 4)
     near = jnp.where(core == 0, 2, 0)
@@ -371,10 +390,7 @@
     )
     own4.start()
 
-    pltpu.make_async_copy(field3, pad.at[far, :, 8:40, :], rz.at[far]).wait()
-    put_rows(far, far * 2)
-    conv(far, False)
-
+    cross(2)
     pltpu.make_async_copy(recv4, recv4, r4).wait()
     for k in range(W):
         even = recv4[pl.ds(k, 4, stride=16), :]
@@ -398,6 +414,10 @@
         tmp3.at[w], tiles_out.at[w * 4 + gy], r3
     )
     own3.start()
+
+    pltpu.make_async_copy(field3, pad.at[far, :, 8:40, :], rz.at[far]).wait()
+    put_rows(far, far * 2)
+    conv(far, False)
 
     grow = (iota((256, C), 0) // 8 == iota((256, C), 1)).astype(F32).astype(BF16)
     grow_t = (iota((C, 256), 1) // 8 == iota((C, 256), 0)).astype(F32).astype(BF16)
@@ -433,8 +453,9 @@
     for dz in (-1, 0, 1):
         for side in range(2):
             copy_row(dz, side).wait_send()
-    for dz in (-1, 1):
-        copy_plane(dz).wait_send()
+    copy_plane(to_near, (0, C)).wait_send()
+    for part in parts:
+        copy_plane(-to_near, part).wait_send()
 
 
 def last_kernel(tiles, point, bias, tyi, txi, out, yh, yl):

time: 53.4 us -> 48 us (0.90)
  Pallas kernels: 53.2 us -> 47.3 us
    pallas_call x1, Pallas kernels: 48.4 us -> 42.5 us  [body(): pl.pallas_call(wide_kernel, name='wide', out_shape=(jax.ShapeDtypeStruct(...]
where the time goes in v4:
time: 48 us; the launch traced here: 47.3 us
  Pallas kernels  47.3 us (99%)
    pallas_call x1, Pallas kernels, body(): pl.pallas_call(wide_kernel, name='wide', out_shape=(jax.ShapeDtypeStruct(...  42.5 us
    pallas_call x1, Pallas kernels, body(): pl.pallas_call(last_kernel, name='last', out_shape=jax.ShapeDtypeStruct((...  4.79 us

profile of v4, /device:TPU:1, one launch (start us, length us, event | category | flops | bytes accessed | tf_op | source)
XLA Modules:
  0.0 47.3 jit_solution(9128480047382084486)
XLA Ops:
  0.0 42.5 %wide.1 = (f32[32,8,128]{2,1,0:T(8,128)}, f32[32,32,256]{2,1,0:T(8,128)}) custom-call(f32[32,32,256]{2,1,0:T(8,128)} %bitcast.7, f32[64,16]{1,0:T(8,128)} %bitcast.8, f32[32,27]{1,0:T(8,128)} %depth_in.1, f32[32,32]{1,0:T(8,128)} %point_in.1, bf16[2,2,256,256]{3,2,1,0:T(8,128)(2,1)} %constant.12.clone.tx_in, f32[4,4,16,256]{3,2,1,0:T(8,128)} %constant.13.clone.ty_in, ...), custom_call_target="tpu_custom_call" | custom-call | tf_op jit(solution)/shard_map/wide/pallas_call | solution.py:523
  42.6 4.8 %last.1 = f32[32,32,256]{2,1,0:T(8,128)} custom-call(f32[32,8,128]{2,1,0:T(8,128)} %get-tuple-element.7.tiles, f32[32,32,256]{2,1,0:T(8,128)} %get-tuple-element.8.point, f32[32]{0:T(128)} %bias.1, f32[4,4,32,128]{3,2,1,0:T(8,128)} %constant.14.clone.tyi, bf16[2,256,512]{2,1,0:T(8,128)(2,1)} %constant.17.clone.txi), custom_call_target="tpu_custom_call" | custom-call | tf_op jit(solution)/shard_map/last/pallas_call | solution.py:569

commit v5 on v4

--- a/solution.py
+++ b/solution.py
@@ -21,7 +21,7 @@
 W = 8
 YL = NY // GY
 VMEM_ALL = 67043328
-CUTS = (8, 22)
+CUTS = (12, 24)
 MESH = pl.DeviceIdType.MESH
 F32 = jnp.float32
 BF16 = jnp.bfloat16
@@ -54,7 +54,8 @@
             np.concatenate([zero, plain, zero, swapped], axis=1),
         ]
     )
-    tables["tx"] = np.stack(halves(tx))
+    high, low = halves(tx)
+    tables["tx"] = np.concatenate([high, high, low], axis=1)
     places = np.arange(NY)
     angle = 2 * np.pi * (kept(MY, NY)[:, None] * places[None, :] % NY) / NY
     parts = []
@@ -78,7 +79,8 @@
     from_s = np.stack([-sin, -cos], axis=1).reshape(64, NX)
     zero = np.zeros_like(from_c)
     txi = np.block([[from_c, zero], [zero, from_c], [from_s, zero], [zero, from_s]])
-    tables["txi"] = np.stack(halves(txi))
+    high, low = halves(txi)
+    tables["txi"] = np.concatenate([high, high, low], axis=0)
     return tables
 
 
@@ -112,9 +114,9 @@
 
 
 def wide_kernel(
-    field3, filt_in, depth_in, point_in, tx_in, ty_in, tz_in, tzi_in,
-    tiles_out, point_out,
-    fv, filt, filt2, depth_w, point_w, tx, ty, tz, tzi,
+    field3, filt_in, depth_in, point_in, tx_in, ty_in, tz_in, tzi_in, tyi_in, txi_in,
+    done_out,
+    fv, filt, filt2, depth_w, point_w, tx, ty, tz, tzi, tyi, txi, wide_yi, recv3,
     pad, edge, hrow, xh, xl, yout, send1, recv1, tmp, send2, recv2, gains,
     send4, recv4, tmp3, depth, pacc,
     ld_sem, s1, r1, sh, rh, sz, rz, s2, r2, s4, r4, s3, r3, so, sf, rf, tokens,
@@ -129,6 +131,11 @@
     def plane_peer(i):
         t = (me + i) % 32
         return (zc * W + t % W, t // W), t
+
+    def plane_loop(step):
+        lax.fori_loop(0, 16, lambda k, carry: step(23 - k, carry), 0)
+        lax.fori_loop(24, 32, step, 0)
+        lax.fori_loop(1, 8, step, 0)
 
     def ring_peer(i):
         return ((zc + i) % ZC) * W + w
@@ -158,6 +165,8 @@
                 (point_in, point_w),
                 (tz_in, tz),
                 (tzi_in, tzi),
+                (tyi_in.at[gy], tyi),
+                (txi_in, txi),
             ]
         )
     ]
@@ -168,7 +177,7 @@
     for dz in (-1, 1):
         for dy in (-1, 0, 1):
             signal(halo_peer(dz, dy))
-    lax.fori_loop(1, 32, greet_plane, 0)
+    plane_loop(greet_plane)
     loads[0].wait()
     for load in loads[3:]:
         load.start()
@@ -185,7 +194,7 @@
                 [fv[4 * s + g] for s in range(8)], axis=0
             )
             high, low = split(rows)
-            value = dot(high, tx[0, ml]) + dot(low, tx[0, ml]) + dot(high, tx[1, ml])
+            value = dot(jnp.concatenate([high, low, high], axis=1), tx[ml])
             total = value if total is None else total + value
         high, low = split(total)
         for part in range(2):
@@ -228,7 +237,7 @@
         copy1(i).start()
         return carry
 
-    lax.fori_loop(1, 32, start1, 0)
+    plane_loop(start1)
     own1 = pltpu.make_async_copy(send1.at[me], recv1.at[me], r1)
     own1.start()
 
@@ -243,8 +252,9 @@
     to_near = 1 - 2 * core
 
     def copy_plane(dz, chans):
+        landed = 1 if chans[0] == CUTS[1] else 1 - dz
         return pltpu.make_async_remote_copy(
-            field3.at[chans[0] : chans[1]], pad.at[1 - dz, chans[0] : chans[1], 8:40, :], sz, rz.at[1 - dz],
+            field3.at[chans[0] : chans[1]], pad.at[1 - dz, chans[0] : chans[1], 8:40, :], sz, rz.at[landed],
             device_id=halo_peer(dz, 0), device_id_type=MESH,
         )
 
@@ -292,7 +302,7 @@
         pad[plane, :, 7, :] = hrow[slot]
         pad[plane, :, 40, :] = hrow[slot + 1]
 
-    def conv(plane, first):
+    def conv(plane, first, chans=(0, C)):
         def channels(step, carry):
             for k in range(4):
                 c = step * 4 + k
@@ -306,7 +316,7 @@
                 depth[c] = value if first else depth[c] + value
             return carry
 
-        lax.fori_loop(0, C // 4, channels, 0)
+        lax.fori_loop(chans[0] // 4, chans[1] // 4, channels, 0)
 
     pl.semaphore_wait(tokens.at[0], 2)
     send_tokens(1, 4)
@@ -361,6 +371,22 @@
     pltpu.make_async_copy(field3, pad.at[near, :, 8:40, :], rz.at[near]).wait()
     put_rows(near, near * 2)
     conv(near, False)
+
+    grow = (iota((256, C), 0) // 8 == iota((256, C), 1)).astype(F32).astype(BF16)
+    grow_t = (iota((C, 256), 1) // 8 == iota((C, 256), 0)).astype(F32).astype(BF16)
+    diagonal = iota((256, 256), 0) % 8 == iota((256, 256), 1) % 8
+    mixers = []
+    for part in split(point_w[...]):
+        tall = dot(grow, part).astype(BF16)
+        mixers.append(jnp.where(diagonal, dot(tall, grow_t), 0.0).astype(BF16))
+    same_i = iota((8, YL, 128), 0) == iota((8, YL, 128), 2) % 8
+    for which in range(4):
+        base = tyi[which]
+        filled = jnp.where(same_i, jnp.broadcast_to(base[None], (8, YL, 128)), 0.0)
+        row = which // 2 * 256
+        filled = filled.reshape(256, 128).astype(BF16)
+        for k in (0, 1) if which % 2 == 0 else (2,):
+            wide_yi[row : row + 256, k * 128 : (k + 1) * 128] = filled
 
     copyf.wait_recv()
     put_gains(filt2, 1 - zc // 8)
@@ -391,6 +417,13 @@
     own4.start()
 
     cross(2)
+    def wait_plane(plane, chans, landed):
+        part = pad.at[plane, chans[0] : chans[1], 8:40, :]
+        pltpu.make_async_copy(part, part, rz.at[landed]).wait()
+
+    wait_plane(far, (0, CUTS[1]), far)
+    put_rows(far, far * 2)
+    conv(far, False, (0, CUTS[1]))
     pltpu.make_async_copy(recv4, recv4, r4).wait()
     for k in range(W):
         even = recv4[pl.ds(k, 4, stride=16), :]
@@ -401,7 +434,7 @@
     def copy3(i):
         target, t = plane_peer(i)
         return pltpu.make_async_remote_copy(
-            tmp3.at[t % W], tiles_out.at[w * 4 + gy], s3, r3,
+            tmp3.at[t % W], recv3.at[w * 4 + gy], s3, r3,
             device_id=target, device_id_type=MESH,
         )
 
@@ -409,32 +442,19 @@
         copy3(i).start()
         return carry
 
-    lax.fori_loop(1, 32, start3, 0)
+    plane_loop(start3)
     own3 = pltpu.make_async_copy(
-        tmp3.at[w], tiles_out.at[w * 4 + gy], r3
+        tmp3.at[w], recv3.at[w * 4 + gy], r3
     )
     own3.start()
 
-    pltpu.make_async_copy(field3, pad.at[far, :, 8:40, :], rz.at[far]).wait()
-    put_rows(far, far * 2)
-    conv(far, False)
-
-    grow = (iota((256, C), 0) // 8 == iota((256, C), 1)).astype(F32).astype(BF16)
-    grow_t = (iota((C, 256), 1) // 8 == iota((C, 256), 0)).astype(F32).astype(BF16)
-    diagonal = iota((256, 256), 0) % 8 == iota((256, 256), 1) % 8
-    mixers = []
-    for part in split(point_w[...]):
-        tall = dot(grow, part).astype(BF16)
-        mixers.append(jnp.where(diagonal, dot(tall, grow_t), 0.0).astype(BF16))
+    wait_plane(far, parts[2], 1)
+    conv(far, False, parts[2])
+
     for k in range(YL // 8):
         d_high, d_low = split(depth[:, k * 8 : (k + 1) * 8, :].reshape(256, NX))
         value = dot(mixers[0], d_high) + dot(mixers[0], d_low) + dot(mixers[1], d_high)
         pacc[:, k * 8 : (k + 1) * 8, :] = value.reshape(C, 8, NX)
-    put = pltpu.make_async_copy(pacc, point_out, so)
-    put.start()
-
-    pltpu.make_async_copy(tiles_out, tiles_out, r3).wait()
-    put.wait()
 
     def done1(i, carry):
         copy1(i).wait_send()
@@ -457,88 +477,77 @@
     for part in parts:
         copy_plane(-to_near, part).wait_send()
 
-
-def last_kernel(tiles, point, bias, tyi, txi, out, yh, yl):
-    step = pl.program_id(0)
-    gy = lax.axis_index("gy")
-
-    @pl.when(step == 0)
-    def _():
-        block = iota((8, 128), 1) // 16 % 4
-        columns = []
+    pltpu.make_async_copy(recv3, recv3, r3).wait()
+    columns = []
+    for p in range(2):
+        rows = []
+        for ky in range(MY):
+            q, k4 = ky // 4, ky % 4
+            value = moved(recv3[p * 16 + q], 0 - k4)
+            for kxb in range(1, 4):
+                value = jnp.where(block == kxb, moved(recv3[(p * 4 + kxb) * 4 + q], kxb - k4), value)
+            rows.append(value)
+        columns.append(jnp.concatenate(rows, axis=0))
+    r_high, r_low = split(jnp.concatenate(columns, axis=1))
+    value = dot(wide_yi[...], jnp.concatenate([r_high, r_low, r_high], axis=0))
+    y_halves = split(value)
+    puts = []
+    for step in range(4):
+
+        def gathered(half):
+            real = half[step * 64 : (step + 1) * 64]
+            imag = half[256 + step * 64 : 256 + (step + 1) * 64]
+            return jnp.concatenate(
+                [
+                    jnp.concatenate(
+                        [real[:, p * 128 : (p + 1) * 128], imag[:, p * 128 : (p + 1) * 128]], axis=1
+                    )
+                    for p in range(2)
+                ],
+                axis=0,
+            )
+
+        high, low = gathered(y_halves[0]), gathered(y_halves[1])
+        spectral = dot(jnp.concatenate([high, low, high], axis=1), txi[...])
         for p in range(2):
-            rows = []
-            for ky in range(MY):
-                q, k4 = ky // 4, ky % 4
-                value = moved(tiles[p * 16 + q], 0 - k4)
-                for kxb in range(1, 4):
-                    value = jnp.where(block == kxb, moved(tiles[(p * 4 + kxb) * 4 + q], kxb - k4), value)
-                rows.append(value)
-            columns.append(jnp.concatenate(rows, axis=0))
-        r_high, r_low = split(jnp.concatenate(columns, axis=1))
-        same = iota((8, YL, 128), 0) == iota((8, YL, 128), 2) % 8
-
-        def spread(which):
-            base = tyi[gy, which]
-            wide = jnp.where(same, jnp.broadcast_to(base[None], (8, YL, 128)), 0.0)
-            return wide.reshape(256, 128).astype(BF16)
-
-        t_high = jnp.concatenate([spread(0), spread(2)], axis=0)
-        t_low = jnp.concatenate([spread(1), spread(3)], axis=0)
-        value = dot(t_high, r_high) + dot(t_high, r_low) + dot(t_low, r_high)
-        high, low = split(value)
-        yh[...] = high
-        yl[...] = low
-
-    def gathered(ref):
-        start = pl.multiple_of(step * 64, 64)
-        real = ref[pl.ds(start, 64), :]
-        imag = ref[pl.ds(256 + start, 64), :]
-        return jnp.concatenate(
-            [
-                jnp.concatenate([real[:, p * 128 : (p + 1) * 128], imag[:, p * 128 : (p + 1) * 128]], axis=1)
-                for p in range(2)
-            ],
-            axis=0,
-        )
-
-    high, low = gathered(yh), gathered(yl)
-    spectral = dot(high, txi[0]) + dot(low, txi[0]) + dot(high, txi[1])
-    for p in range(2):
-        for sl in range(2):
-            for ml in range(2):
-                ch = 4 * sl + 2 * ml + p
-                value = spectral[p * 64 + sl * 32 : p * 64 + (sl + 1) * 32, ml * 256 : (ml + 1) * 256]
-                value = value + point[ch] + bias[step * 8 + ch]
-                out[ch] = 0.5 * value * (1.0 + lax.erf(value * (0.5**0.5)))
+            for sl in range(2):
+                for ml in range(2):
+                    ch = step * 8 + 4 * sl + 2 * ml + p
+                    row = p * 64 + sl * 32
+                    pacc[ch] = pacc[ch] + spectral[row : row + 32, ml * 256 : (ml + 1) * 256]
+        chans = pl.ds(step * 8, 8)
+        put = pltpu.make_async_copy(pacc.at[chans], done_out.at[chans], so.at[step])
+        put.start()
+        puts.append(put)
+    for put in puts:
+        put.wait()
 
 
 def body(field, spectral_filter, depth_weight, point_weight, bias_vector):
     field3 = field.reshape(C, YL, NX)
     filt = spectral_filter.transpose(0, 2, 3, 1).reshape(64, 16)
     const = {name: jnp.asarray(value) for name, value in TABLES.items()}
-    vmem = pl.BlockSpec(memory_space=pltpu.VMEM)
-    smem = pl.BlockSpec(memory_space=pltpu.SMEM)
     hbm = pl.BlockSpec(memory_space=pltpu.HBM)
-    tiles, point = pl.pallas_call(
+    value = pl.pallas_call(
         wide_kernel,
         name="wide",
-        out_shape=(
-            jax.ShapeDtypeStruct((32, 8, 128), F32),
-            jax.ShapeDtypeStruct((C, YL, NX), F32),
-        ),
-        in_specs=[hbm] * 8,
-        out_specs=(hbm, hbm),
+        out_shape=jax.ShapeDtypeStruct((C, YL, NX), F32),
+        in_specs=[hbm] * 10,
+        out_specs=hbm,
         scratch_shapes=[
             VMEM((C, YL, NX), F32),
             VMEM((64, 16), F32),
             VMEM((64, 16), F32),
             pltpu.SMEM((C, 27), F32),
             VMEM((C, C), F32),
-            VMEM((2, 2, 256, 256), BF16),
+            VMEM((2, 768, 256), BF16),
             VMEM((4, MY, 256), F32),
             VMEM((64, 128), BF16),
             VMEM((256, 32), BF16),
+            VMEM((4, YL, 128), F32),
+            VMEM((768, 512), BF16),
+            VMEM((512, 384), BF16),
+            VMEM((32, 8, 128), F32),
             VMEM((3, C, 48, NX), F32),
             VMEM((2, C, NX), F32),
             VMEM((6, C, NX), F32),
@@ -556,7 +565,7 @@
             VMEM((W, 8, 128), F32),
             VMEM((C, YL, NX), F32),
             VMEM((C, YL, NX), F32),
-            DMA((9,)), DMA, DMA, DMA, DMA((2,)), DMA, DMA((3,)), DMA, DMA, DMA, DMA, DMA, DMA, DMA, DMA, DMA,
+            DMA((11,)), DMA, DMA, DMA, DMA((2,)), DMA, DMA((3,)), DMA, DMA, DMA, DMA, DMA, DMA, DMA((4,)), DMA, DMA,
             pltpu.SemaphoreType.REGULAR((2,)),
         ],
         compiler_params=pltpu.CompilerParams(
@@ -564,25 +573,10 @@
         ),
     )(
         field3, filt, depth_weight, point_weight,
-        const["tx"], const["ty"], const["tz"], const["tzi"],
+        const["tx"], const["ty"], const["tz"], const["tzi"], const["tyi"], const["txi"],
     )
-    out = pl.pallas_call(
-        last_kernel,
-        name="last",
-        out_shape=jax.ShapeDtypeStruct((C, YL, NX), F32),
-        grid=(4,),
-        in_specs=[
-            vmem,
-            pl.BlockSpec((8, YL, NX), lambda i: (i, 0, 0)),
-            smem,
-            vmem,
-            vmem,
-        ],
-        out_specs=pl.BlockSpec((8, YL, NX), lambda i: (i, 0, 0)),
-        scratch_shapes=[VMEM((512, 256), BF16), VMEM((512, 256), BF16)],
-        compiler_params=pltpu.CompilerParams(dimension_semantics=("arbitrary",), vmem_limit_bytes=VMEM_ALL),
-    )(tiles, point, bias_vector, const["tyi"], const["txi"])
-    return out.reshape(C, 1, YL, NX)
+    value = value.reshape(C, 1, YL, NX) + bias_vector[:, None, None, None]
+    return 0.5 * value * (1.0 + lax.erf(value * (0.5**0.5)))
 
 
 def solution(mesh):

time: 48 us -> 46.8 us (0.975)
  Pallas kernels: 47.3 us -> 44.1 us
  other arithmetic: 0 us -> 2.47 us
    pallas_call x2 -> x1, Pallas kernels: 47.3 us -> 44.1 us  [body(): pl.pallas_call(wide_kernel, name='wide', out_shape=jax.ShapeDtypeStruct((...]
    mul x0 -> x1, other arithmetic: none -> 2.47 us  [body(): return 0.5 * value * (1.0 + lax.erf(value * 0.5 ** 0.5))]
where the time goes in v5:
time: 46.8 us; the launch traced here: 46.6 us
  Pallas kernels  44.1 us (94%)
  other arithmetic  2.47 us (5%)
    pallas_call x1, Pallas kernels, body(): pl.pallas_call(wide_kernel, name='wide', out_shape=jax.ShapeDtypeStruct((...  44.1 us
    mul x1, other arithmetic, body(): return 0.5 * value * (1.0 + lax.erf(value * 0.5 ** 0.5))  2.47 us

profile of v5, /device:TPU:1, one launch (start us, length us, event | category | flops | bytes accessed | tf_op | source)
XLA Modules:
  0.0 46.6 jit_solution(18376238629794319755)
XLA Ops:
  0.0 44.1 %wide.1 = f32[32,32,256]{2,1,0:T(8,128)} custom-call(f32[32,32,256]{2,1,0:T(8,128)} %bitcast.8, f32[64,16]{1,0:T(8,128)} %bitcast.9, f32[32,27]{1,0:T(8,128)} %depth_in.1, f32[32,32]{1,0:T(8,128)} %point_in.1, bf16[2,768,256]{2,1,0:T(8,128)(2,1)} %constant.18.clone.tx_in, f32[4,4,16,256]{3,2,1,0:T(8,128)} %constant.19.clone.ty_in, ...), custom_call_target="tpu_custom_call" | custom-call | tf_op jit(solution)/shard_map/wide/pallas_call | solution.py:531
  44.1 2.5 %multiply_bitcast_fusion = f32[32,1,32,256]{3,2,1,0:T(8,128)} fusion(f32[32,32,256]{2,1,0:T(8,128)} %wide.1, f32[32]{0:T(128)} %param.15), kind=kLoop, calls=%fused_computation | loop fusion | flops 1310720 | bytes 2097280 | tf_op jit(solution)/shard_map/mul | solution.py:579

commit v6 on v5

--- a/solution.py
+++ b/solution.py
@@ -67,10 +67,12 @@
     tables["tyi"] = np.repeat(mine.transpose(0, 1, 3, 2), 8, axis=3)
     angle = 2 * np.pi * (kept(MZ, NZ)[:, None] * np.arange(NZ)[None, :] % NZ) / NZ
     high, low = halves(np.concatenate([np.cos(angle), np.sin(angle)], axis=0))
-    tables["tz"] = np.concatenate([high, low], axis=0)
+    both = np.concatenate([high, low], axis=0)
+    tables["tz"] = np.concatenate([both, both], axis=1)
     scale = (NX * NY * NZ) ** -0.5 * (2.0 * MX * MY * MZ) ** -0.5
     both = np.concatenate([np.cos(angle), np.sin(angle)], axis=0).T * scale
-    tables["tzi"] = np.concatenate(halves(both), axis=0)
+    both = np.concatenate(halves(both), axis=0)
+    tables["tzi"] = np.concatenate([both, both], axis=1)
     weight = np.where(np.arange(MX) == 0, 1.0, 2.0)[:, None]
     angle = 2 * np.pi * (np.arange(MX)[:, None] * np.arange(NX)[None, :] % NX) / NX
     cos = (weight * np.cos(angle)).reshape(4, 8, NX)
@@ -114,43 +116,40 @@
 
 
 def wide_kernel(
-    field3, filt_in, depth_in, point_in, tx_in, ty_in, tz_in, tzi_in, tyi_in, txi_in,
-    done_out,
-    fv, filt, filt2, depth_w, point_w, tx, ty, tz, tzi, tyi, txi, wide_yi, recv3,
+    field3, filt_in, depth_in, point_in, tx_in, ty_in, tz_in, tzi_in,
+    recv3, point_out,
+    fv, filt, filt2, depth_w, point_w, tx, ty, tz, tzi,
     pad, edge, hrow, xh, xl, yout, send1, recv1, tmp, send2, recv2, gains,
     send4, recv4, tmp3, depth, pacc,
     ld_sem, s1, r1, sh, rh, sz, rz, s2, r2, s4, r4, s3, r3, so, sf, rf, tokens,
 ):
     gz = lax.axis_index("gz")
     gy = lax.axis_index("gy")
-    zc = gz // W
-    w = gz % W
-    core = gz % 2
+    zc = lax.div(gz, W)
+    w = lax.rem(gz, W)
+    core = lax.rem(gz, 2)
     me = gy * W + w
 
-    def plane_peer(i):
-        t = (me + i) % 32
-        return (zc * W + t % W, t // W), t
-
-    def plane_loop(step):
-        lax.fori_loop(0, 16, lambda k, carry: step(23 - k, carry), 0)
-        lax.fori_loop(24, 32, step, 0)
-        lax.fori_loop(1, 8, step, 0)
+    ws = [w] + [lax.rem(w + k, W) for k in range(1, W)]
+    gys = [gy] + [lax.rem(gy + k, GY) for k in range(1, GY)]
+    zs = [zc] + [lax.rem(zc + k, ZC) for k in range(1, ZC)]
+    first_gz = gz - w
+    plane_peers = [(dx, dw) for dx in (2, 1, 3, 0) for dw in (4, 3, 5, 2, 6, 1, 7, 0) if dx or dw]
+
+    def plane_peer(peer):
+        dx, dw = peer
+        return (first_gz + ws[dw], gys[dx]), gys[dx] * W + ws[dw]
 
     def ring_peer(i):
-        return ((zc + i) % ZC) * W + w
+        return zs[i] * W + w
 
     def halo_peer(dz, dy):
-        return ((gz + NZ + dz) % NZ, (gy + GY + dy) % GY)
+        return (lax.rem(gz + (NZ + dz), NZ), gys[dy % GY])
 
     barrier = pltpu.get_barrier_semaphore()
 
     def signal(target):
         pl.semaphore_signal(barrier, inc=1, device_id=target, device_id_type=MESH)
-
-    def greet_plane(i, carry):
-        signal(plane_peer(i)[0])
-        return carry
 
     loads = [
         pltpu.make_async_copy(src, dst, ld_sem.at[k])
@@ -165,8 +164,6 @@
                 (point_in, point_w),
                 (tz_in, tz),
                 (tzi_in, tzi),
-                (tyi_in.at[gy], tyi),
-                (txi_in, txi),
             ]
         )
     ]
@@ -177,7 +174,8 @@
     for dz in (-1, 1):
         for dy in (-1, 0, 1):
             signal(halo_peer(dz, dy))
-    plane_loop(greet_plane)
+    for peer in plane_peers:
+        signal(plane_peer(peer)[0])
     loads[0].wait()
     for load in loads[3:]:
         load.start()
@@ -233,11 +231,8 @@
             send1.at[t], recv1.at[me], s1, r1, device_id=target, device_id_type=MESH
         )
 
-    def start1(i, carry):
-        copy1(i).start()
-        return carry
-
-    plane_loop(start1)
+    for peer in plane_peers:
+        copy1(peer).start()
     own1 = pltpu.make_async_copy(send1.at[me], recv1.at[me], r1)
     own1.start()
 
@@ -252,7 +247,7 @@
     to_near = 1 - 2 * core
 
     def copy_plane(dz, chans):
-        landed = 1 if chans[0] == CUTS[1] else 1 - dz
+        landed = 1 - dz if chans[0] == 0 else 1
         return pltpu.make_async_remote_copy(
             field3.at[chans[0] : chans[1]], pad.at[1 - dz, chans[0] : chans[1], 8:40, :], sz, rz.at[landed],
             device_id=halo_peer(dz, 0), device_id_type=MESH,
@@ -296,7 +291,7 @@
     for load in loads[4:]:
         load.wait()
     gains[...] = jnp.zeros_like(gains)
-    put_gains(filt, zc // 8)
+    put_gains(filt, lax.div(zc, 8))
 
     def put_rows(plane, slot):
         pad[plane, :, 7, :] = hrow[slot]
@@ -333,25 +328,22 @@
         else:
             send2[k] = jnp.where(lower, pltpu.roll(one, 64, 1), two)
 
+    far_first = (8, 7, 9, 6, 10, 5, 11, 4, 12, 3, 13, 2, 14, 1, 15)
     pl.semaphore_wait(tokens.at[1], 2)
 
-    def copy2(k):
-        i = 8 + (k + 1) // 2 * (2 * (k % 2) - 1)
+    def copy2(i):
         return pltpu.make_async_remote_copy(
-            send2.at[(zc + i) % 8], recv2.at[zc], s2, r2,
+            send2.at[lax.rem(zs[i], 8)], recv2.at[zc], s2, r2,
             device_id=(ring_peer(i), gy), device_id_type=MESH,
         )
-
-    def start2(k, carry):
-        copy2(k).start()
-        return carry
 
     copyf = pltpu.make_async_remote_copy(
         filt_in, filt2, sf, rf, device_id=(ring_peer(8), gy), device_id_type=MESH
     )
     copyf.start()
-    lax.fori_loop(0, ZC - 1, start2, 0)
-    own2 = pltpu.make_async_copy(send2.at[zc % 8], recv2.at[zc], r2)
+    for i in far_first:
+        copy2(i).start()
+    own2 = pltpu.make_async_copy(send2.at[lax.rem(zc, 8)], recv2.at[zc], r2)
     own2.start()
 
     cross(1)
@@ -379,32 +371,23 @@
     for part in split(point_w[...]):
         tall = dot(grow, part).astype(BF16)
         mixers.append(jnp.where(diagonal, dot(tall, grow_t), 0.0).astype(BF16))
-    same_i = iota((8, YL, 128), 0) == iota((8, YL, 128), 2) % 8
-    for which in range(4):
-        base = tyi[which]
-        filled = jnp.where(same_i, jnp.broadcast_to(base[None], (8, YL, 128)), 0.0)
-        row = which // 2 * 256
-        filled = filled.reshape(256, 128).astype(BF16)
-        for k in (0, 1) if which % 2 == 0 else (2,):
-            wide_yi[row : row + 256, k * 128 : (k + 1) * 128] = filled
-
     copyf.wait_recv()
-    put_gains(filt2, 1 - zc // 8)
+    put_gains(filt2, 1 - lax.div(zc, 8))
     gain_re = jnp.transpose(gains[0])[0:16, :]
     gain_im = jnp.transpose(gains[1])[0:16, :]
     pltpu.make_async_copy(recv2, recv2, r2).wait()
     a_high, a_low = split(recv2[...].reshape(NZ, 128))
-    both = dot(tz[...], a_high) + dot(tz[...], a_low)
+    both = dot(tz[...], jnp.concatenate([a_high, a_low], axis=0))
     modes = both[0:16] + both[32:48] + swapped(both[16:32] + both[48:64])
     filtered = modes * gain_re - swapped(modes) * gain_im
     stacked = jnp.concatenate([filtered, -swapped(filtered)], axis=0)
     f_high, f_low = split(stacked)
-    both = dot(tzi[...], f_high) + dot(tzi[...], f_low)
+    both = dot(tzi[...], jnp.concatenate([f_high, f_low], axis=0))
     send4[...] = (both[0:128] + both[128:256]).reshape(ZC, 8, 128)
 
     def copy4(i):
         return pltpu.make_async_remote_copy(
-            send4.at[(zc + i) % ZC], recv4.at[pl.ds(pl.multiple_of(zc % 8 * 8, 8), 8), :], s4, r4,
+            send4.at[zs[i]], recv4.at[pl.ds(pl.multiple_of(lax.rem(zc, 8) * 8, 8), 8), :], s4, r4,
             device_id=(ring_peer(i), gy), device_id_type=MESH,
         )
 
@@ -412,7 +395,7 @@
     for i in nearer:
         copy4(i).start()
     own4 = pltpu.make_async_copy(
-        send4.at[zc], recv4.at[pl.ds(pl.multiple_of(zc % 8 * 8, 8), 8), :], r4
+        send4.at[zc], recv4.at[pl.ds(pl.multiple_of(lax.rem(zc, 8) * 8, 8), 8), :], r4
     )
     own4.start()
 
@@ -421,9 +404,9 @@
         part = pad.at[plane, chans[0] : chans[1], 8:40, :]
         pltpu.make_async_copy(part, part, rz.at[landed]).wait()
 
-    wait_plane(far, (0, CUTS[1]), far)
+    wait_plane(far, parts[0], far)
     put_rows(far, far * 2)
-    conv(far, False, (0, CUTS[1]))
+    conv(far, False, parts[0])
     pltpu.make_async_copy(recv4, recv4, r4).wait()
     for k in range(W):
         even = recv4[pl.ds(k, 4, stride=16), :]
@@ -434,39 +417,32 @@
     def copy3(i):
         target, t = plane_peer(i)
         return pltpu.make_async_remote_copy(
-            tmp3.at[t % W], recv3.at[w * 4 + gy], s3, r3,
+            tmp3.at[ws[i[1]]], recv3.at[w * 4 + gy], s3, r3,
             device_id=target, device_id_type=MESH,
         )
 
-    def start3(i, carry):
-        copy3(i).start()
-        return carry
-
-    plane_loop(start3)
+    for peer in plane_peers:
+        copy3(peer).start()
     own3 = pltpu.make_async_copy(
         tmp3.at[w], recv3.at[w * 4 + gy], r3
     )
     own3.start()
 
-    wait_plane(far, parts[2], 1)
-    conv(far, False, parts[2])
+    wait_plane(far, (CUTS[0], C), 1)
+    conv(far, False, (CUTS[0], C))
 
     for k in range(YL // 8):
         d_high, d_low = split(depth[:, k * 8 : (k + 1) * 8, :].reshape(256, NX))
         value = dot(mixers[0], d_high) + dot(mixers[0], d_low) + dot(mixers[1], d_high)
         pacc[:, k * 8 : (k + 1) * 8, :] = value.reshape(C, 8, NX)
-
-    def done1(i, carry):
-        copy1(i).wait_send()
-        copy3(i).wait_send()
-        return carry
-
-    def done2(k, carry):
-        copy2(k).wait_send()
-        return carry
-
-    lax.fori_loop(1, 32, done1, 0)
-    lax.fori_loop(0, ZC - 1, done2, 0)
+    put = pltpu.make_async_copy(pacc, point_out, so)
+    put.start()
+
+    for peer in plane_peers:
+        copy1(peer).wait_send()
+        copy3(peer).wait_send()
+    for i in far_first:
+        copy2(i).wait_send()
     for i in nearer:
         copy4(i).wait_send()
     copyf.wait_send()
@@ -478,21 +454,55 @@
         copy_plane(-to_near, part).wait_send()
 
     pltpu.make_async_copy(recv3, recv3, r3).wait()
+    put.wait()
+
+
+def last_kernel(
+    tiles_in, point_in, tyi_in, txi_in, bias_in, done_out,
+    tiles, point, tyi, txi, bias, wide_yi, ld_sem, pt_sem, so,
+):
+    gy = lax.axis_index("gy")
+    loads = [
+        pltpu.make_async_copy(src, dst, ld_sem.at[k])
+        for k, (src, dst) in enumerate(
+            [(tyi_in.at[gy], tyi), (tiles_in, tiles), (bias_in, bias), (txi_in, txi)]
+        )
+    ]
+    quarters = [pl.ds(k * 8, 8) for k in range(4)]
+    points = [
+        pltpu.make_async_copy(point_in.at[q], point.at[q], pt_sem.at[k]) for k, q in enumerate(quarters)
+    ]
+    for load in loads + points:
+        load.start()
+    block = iota((8, 128), 1) // 16 % 4
+    same_i = iota((8, YL, 128), 0) == iota((8, YL, 128), 2) % 8
+    loads[0].wait()
+    for which in range(4):
+        base = tyi[which]
+        filled = jnp.where(same_i, jnp.broadcast_to(base[None], (8, YL, 128)), 0.0)
+        row = which // 2 * 256
+        filled = filled.reshape(256, 128).astype(BF16)
+        for k in (0, 1) if which % 2 == 0 else (2,):
+            wide_yi[row : row + 256, k * 128 : (k + 1) * 128] = filled
+    loads[1].wait()
+    loads[2].wait()
     columns = []
     for p in range(2):
         rows = []
         for ky in range(MY):
             q, k4 = ky // 4, ky % 4
-            value = moved(recv3[p * 16 + q], 0 - k4)
+            value = moved(tiles[p * 16 + q], 0 - k4)
             for kxb in range(1, 4):
-                value = jnp.where(block == kxb, moved(recv3[(p * 4 + kxb) * 4 + q], kxb - k4), value)
+                value = jnp.where(block == kxb, moved(tiles[(p * 4 + kxb) * 4 + q], kxb - k4), value)
             rows.append(value)
         columns.append(jnp.concatenate(rows, axis=0))
     r_high, r_low = split(jnp.concatenate(columns, axis=1))
     value = dot(wide_yi[...], jnp.concatenate([r_high, r_low, r_high], axis=0))
     y_halves = split(value)
+    loads[3].wait()
     puts = []
     for step in range(4):
+        points[step].wait()
 
         def gathered(half):
             real = half[step * 64 : (step + 1) * 64]
@@ -514,9 +524,10 @@
                 for ml in range(2):
                     ch = step * 8 + 4 * sl + 2 * ml + p
                     row = p * 64 + sl * 32
-                    pacc[ch] = pacc[ch] + spectral[row : row + 32, ml * 256 : (ml + 1) * 256]
+                    value = point[ch] + spectral[row : row + 32, ml * 256 : (ml + 1) * 256] + bias[0, ch]
+                    point[ch] = 0.5 * value * (1.0 + lax.erf(value * (0.5**0.5)))
         chans = pl.ds(step * 8, 8)
-        put = pltpu.make_async_copy(pacc.at[chans], done_out.at[chans], so.at[step])
+        put = pltpu.make_async_copy(point.at[chans], done_out.at[chans], so.at[step])
         put.start()
         puts.append(put)
     for put in puts:
@@ -528,12 +539,15 @@
     filt = spectral_filter.transpose(0, 2, 3, 1).reshape(64, 16)
     const = {name: jnp.asarray(value) for name, value in TABLES.items()}
     hbm = pl.BlockSpec(memory_space=pltpu.HBM)
-    value = pl.pallas_call(
+    tiles, point = pl.pallas_call(
         wide_kernel,
         name="wide",
-        out_shape=jax.ShapeDtypeStruct((C, YL, NX), F32),
-        in_specs=[hbm] * 10,
-        out_specs=hbm,
+        out_shape=(
+            jax.ShapeDtypeStruct((32, 8, 128), F32),
+            jax.ShapeDtypeStruct((C, YL, NX), F32),
+        ),
+        in_specs=[hbm] * 8,
+        out_specs=(hbm, hbm),
         scratch_shapes=[
             VMEM((C, YL, NX), F32),
             VMEM((64, 16), F32),
@@ -542,12 +556,8 @@
             VMEM((C, C), F32),
             VMEM((2, 768, 256), BF16),
             VMEM((4, MY, 256), F32),
-            VMEM((64, 128), BF16),
-            VMEM((256, 32), BF16),
-            VMEM((4, YL, 128), F32),
-            VMEM((768, 512), BF16),
-            VMEM((512, 384), BF16),
-            VMEM((32, 8, 128), F32),
+            VMEM((64, 256), BF16),
+            VMEM((256, 64), BF16),
             VMEM((3, C, 48, NX), F32),
             VMEM((2, C, NX), F32),
             VMEM((6, C, NX), F32),
@@ -565,7 +575,7 @@
             VMEM((W, 8, 128), F32),
             VMEM((C, YL, NX), F32),
             VMEM((C, YL, NX), F32),
-            DMA((11,)), DMA, DMA, DMA, DMA((2,)), DMA, DMA((3,)), DMA, DMA, DMA, DMA, DMA, DMA, DMA((4,)), DMA, DMA,
+            DMA((9,)), DMA, DMA, DMA, DMA((2,)), DMA, DMA((3,)), DMA, DMA, DMA, DMA, DMA, DMA, DMA, DMA, DMA,
             pltpu.SemaphoreType.REGULAR((2,)),
         ],
         compiler_params=pltpu.CompilerParams(
@@ -573,10 +583,26 @@
         ),
     )(
         field3, filt, depth_weight, point_weight,
-        const["tx"], const["ty"], const["tz"], const["tzi"], const["tyi"], const["txi"],
+        const["tx"], const["ty"], const["tz"], const["tzi"],
     )
-    value = value.reshape(C, 1, YL, NX) + bias_vector[:, None, None, None]
-    return 0.5 * value * (1.0 + lax.erf(value * (0.5**0.5)))
+    value = pl.pallas_call(
+        last_kernel,
+        name="last",
+        out_shape=jax.ShapeDtypeStruct((C, YL, NX), F32),
+        in_specs=[hbm] * 5,
+        out_specs=hbm,
+        scratch_shapes=[
+            VMEM((32, 8, 128), F32),
+            VMEM((C, YL, NX), F32),
+            VMEM((4, YL, 128), F32),
+            VMEM((768, 512), BF16),
+            pltpu.SMEM((1, C), F32),
+            VMEM((512, 384), BF16),
+            DMA((4,)), DMA((4,)), DMA((4,)),
+        ],
+        compiler_params=pltpu.CompilerParams(vmem_limit_bytes=VMEM_ALL),
+    )(tiles, point, const["tyi"], const["txi"], bias_vector.reshape(1, C))
+    return value.reshape(C, 1, YL, NX)
 
 
 def solution(mesh):

time: 46.8 us -> 45.1 us (0.964)
  other arithmetic: 2.47 us -> 0 us
  Pallas kernels: 44.1 us -> 45 us
    mul x1 -> x0, other arithmetic: 2.47 us -> none  [body(): return 0.5 * value * (1.0 + lax.erf(value * 0.5 ** 0.5))]
    pallas_call x1 -> x2, Pallas kernels: 44.1 us -> 45 us  [the longest x1 41.2 us: body(): pl.pallas_call(wide_kernel, name='wide', out_shape=(jax.ShapeDtypeStruct(...]
where the time goes in v6:
time: 45.1 us; the launch traced here: 45 us
  Pallas kernels  45 us (100%)
    pallas_call x1, Pallas kernels, body(): pl.pallas_call(wide_kernel, name='wide', out_shape=(jax.ShapeDtypeStruct(...  41.2 us
    pallas_call x1, Pallas kernels, body(): pl.pallas_call(last_kernel, name='last', out_shape=jax.ShapeDtypeStruct((...  3.74 us

profile of v6, /device:TPU:1, one launch (start us, length us, event | category | flops | bytes accessed | tf_op | source)
XLA Modules:
  0.0 45.0 jit_solution(14076642248064774743)
XLA Ops:
  0.0 41.2 %wide.1 = (f32[32,8,128]{2,1,0:T(8,128)}, f32[32,32,256]{2,1,0:T(8,128)}) custom-call(f32[32,32,256]{2,1,0:T(8,128)} %bitcast.8, f32[64,16]{1,0:T(8,128)} %bitcast.9, f32[32,27]{1,0:T(8,128)} %depth_in.1, f32[32,32]{1,0:T(8,128)} %point_in.1, bf16[2,768,256]{2,1,0:T(8,128)(2,1)} %constant.12.clone.tx_in, f32[4,4,16,256]{3,2,1,0:T(8,128)} %constant.13.clone.ty_in, ...), custom_call_target="tpu_custom_call" | custom-call | tf_op jit(solution)/shard_map/wide/pallas_call | solution.py:542
  41.2 3.7 %last.1 = f32[32,32,256]{2,1,0:T(8,128)} custom-call(f32[32,8,128]{2,1,0:T(8,128)} %get-tuple-element.7.tiles_in, f32[32,32,256]{2,1,0:T(8,128)} %get-tuple-element.8.point_in, f32[4,4,32,128]{3,2,1,0:T(8,128)} %constant.14.clone.tyi_in, bf16[768,512]{1,0:T(8,128)(2,1)} %constant.17.clone.txi_in, f32[1,32]{1,0:T(1,128)} %bitcast.10), custom_call_target="tpu_custom_call" | custom-call | tf_op jit(solution)/shard_map/last/pallas_call | solution.py:588

commit v7 on v6

--- a/solution.py
+++ b/solution.py
@@ -21,7 +21,7 @@
 W = 8
 YL = NY // GY
 VMEM_ALL = 67043328
-CUTS = (12, 24)
+CUTS = (8, 24)
 MESH = pl.DeviceIdType.MESH
 F32 = jnp.float32
 BF16 = jnp.bfloat16
@@ -118,7 +118,7 @@
 def wide_kernel(
     field3, filt_in, depth_in, point_in, tx_in, ty_in, tz_in, tzi_in,
     recv3, point_out,
-    fv, filt, filt2, depth_w, point_w, tx, ty, tz, tzi,
+    fv, filt, fwide, ftile, ftile2, depth_w, point_w, tx, ty, tz, tzi,
     pad, edge, hrow, xh, xl, yout, send1, recv1, tmp, send2, recv2, gains,
     send4, recv4, tmp3, depth, pacc,
     ld_sem, s1, r1, sh, rh, sz, rz, s2, r2, s4, r4, s3, r3, so, sf, rf, tokens,
@@ -281,17 +281,24 @@
     for dz in (-1, 1):
         for side in range(2):
             copy_row(dz, side).start()
-    def put_gains(source, pair):
+    def put_gains(tile, pair):
         for part in range(2):
             for ky in range(4):
+                k = part * 4 + ky
+                value = tile if k == 0 else pltpu.roll(tile, 128 - k * 16, 1)
                 for r in range(2):
                     row = pl.multiple_of(pair * 64 + ky * 16 + r * 8, 8)
-                    gains[part, pl.ds(row, 8), 0:16] = source[part * 32 + ky * 8 : part * 32 + ky * 8 + 8, :]
+                    gains[part, pl.ds(row, 8), :] = value
 
     for load in loads[4:]:
         load.wait()
-    gains[...] = jnp.zeros_like(gains)
-    put_gains(filt, lax.div(zc, 8))
+    fwide[:, 0:16] = filt[...]
+    tile = fwide[0:8, :]
+    for k in range(1, 8):
+        moved_in = pltpu.roll(fwide[k * 8 : k * 8 + 8, :], k * 16, 1)
+        tile = jnp.where(iota((8, 128), 1) // 16 == k, moved_in, tile)
+    ftile[...] = tile
+    put_gains(tile, lax.div(zc, 8))
 
     def put_rows(plane, slot):
         pad[plane, :, 7, :] = hrow[slot]
@@ -338,7 +345,7 @@
         )
 
     copyf = pltpu.make_async_remote_copy(
-        filt_in, filt2, sf, rf, device_id=(ring_peer(8), gy), device_id_type=MESH
+        ftile, ftile2, sf, rf, device_id=(ring_peer(8), gy), device_id_type=MESH
     )
     copyf.start()
     for i in far_first:
@@ -372,7 +379,7 @@
         tall = dot(grow, part).astype(BF16)
         mixers.append(jnp.where(diagonal, dot(tall, grow_t), 0.0).astype(BF16))
     copyf.wait_recv()
-    put_gains(filt2, 1 - lax.div(zc, 8))
+    put_gains(ftile2[...], 1 - lax.div(zc, 8))
     gain_re = jnp.transpose(gains[0])[0:16, :]
     gain_im = jnp.transpose(gains[1])[0:16, :]
     pltpu.make_async_copy(recv2, recv2, r2).wait()
@@ -551,7 +558,9 @@
         scratch_shapes=[
             VMEM((C, YL, NX), F32),
             VMEM((64, 16), F32),
-            VMEM((64, 16), F32),
+            VMEM((64, 128), F32),
+            VMEM((8, 128), F32),
+            VMEM((8, 128), F32),
             pltpu.SMEM((C, 27), F32),
             VMEM((C, C), F32),
             VMEM((2, 768, 256), BF16),

time: 45.1 us -> 42.5 us (0.942)
  Pallas kernels: 45 us -> 42.4 us
    pallas_call x1, Pallas kernels: 41.2 us -> 38.6 us  [body(): pl.pallas_call(wide_kernel, name='wide', out_shape=(jax.ShapeDtypeStruct(...]
where the time goes in v7:
time: 42.5 us; the launch traced here: 42.4 us
  Pallas kernels  42.4 us (100%)
    pallas_call x1, Pallas kernels, body(): pl.pallas_call(wide_kernel, name='wide', out_shape=(jax.ShapeDtypeStruct(...  38.6 us
    pallas_call x1, Pallas kernels, body(): pl.pallas_call(last_kernel, name='last', out_shape=jax.ShapeDtypeStruct((...  3.74 us

profile of v7, /device:TPU:1, one launch (start us, length us, event | category | flops | bytes accessed | tf_op | source)
XLA Modules:
  0.0 42.4 jit_solution(3102802624456776606)
XLA Ops:
  0.0 38.6 %wide.1 = (f32[32,8,128]{2,1,0:T(8,128)}, f32[32,32,256]{2,1,0:T(8,128)}) custom-call(f32[32,32,256]{2,1,0:T(8,128)} %bitcast.8, f32[64,16]{1,0:T(8,128)} %bitcast.9, f32[32,27]{1,0:T(8,128)} %depth_in.1, f32[32,32]{1,0:T(8,128)} %point_in.1, bf16[2,768,256]{2,1,0:T(8,128)(2,1)} %constant.12.clone.tx_in, f32[4,4,16,256]{3,2,1,0:T(8,128)} %constant.13.clone.ty_in, ...), custom_call_target="tpu_custom_call" | custom-call | tf_op jit(solution)/shard_map/wide/pallas_call | solution.py:549
  38.6 3.7 %last.1 = f32[32,32,256]{2,1,0:T(8,128)} custom-call(f32[32,8,128]{2,1,0:T(8,128)} %get-tuple-element.7.tiles_in, f32[32,32,256]{2,1,0:T(8,128)} %get-tuple-element.8.point_in, f32[4,4,32,128]{3,2,1,0:T(8,128)} %constant.14.clone.tyi_in, bf16[768,512]{1,0:T(8,128)(2,1)} %constant.17.clone.txi_in, f32[1,32]{1,0:T(1,128)} %bitcast.10), custom_call_target="tpu_custom_call" | custom-call | tf_op jit(solution)/shard_map/last/pallas_call | solution.py:597

commit v8 on v7

--- a/solution.py
+++ b/solution.py
@@ -247,7 +247,7 @@
     to_near = 1 - 2 * core
 
     def copy_plane(dz, chans):
-        landed = 1 - dz if chans[0] == 0 else 1
+        landed = {0: 1 - dz, CUTS[0]: 3, CUTS[1]: 1}[chans[0]]
         return pltpu.make_async_remote_copy(
             field3.at[chans[0] : chans[1]], pad.at[1 - dz, chans[0] : chans[1], 8:40, :], sz, rz.at[landed],
             device_id=halo_peer(dz, 0), device_id_type=MESH,
@@ -435,8 +435,10 @@
     )
     own3.start()
 
-    wait_plane(far, (CUTS[0], C), 1)
-    conv(far, False, (CUTS[0], C))
+    wait_plane(far, parts[1], 3)
+    conv(far, False, parts[1])
+    wait_plane(far, parts[2], 1)
+    conv(far, False, parts[2])
 
     for k in range(YL // 8):
         d_high, d_low = split(depth[:, k * 8 : (k + 1) * 8, :].reshape(256, NX))
@@ -584,7 +586,7 @@
             VMEM((W, 8, 128), F32),
             VMEM((C, YL, NX), F32),
             VMEM((C, YL, NX), F32),
-            DMA((9,)), DMA, DMA, DMA, DMA((2,)), DMA, DMA((3,)), DMA, DMA, DMA, DMA, DMA, DMA, DMA, DMA, DMA,
+            DMA((9,)), DMA, DMA, DMA, DMA((2,)), DMA, DMA((4,)), DMA, DMA, DMA, DMA, DMA, DMA, DMA, DMA, DMA,
             pltpu.SemaphoreType.REGULAR((2,)),
         ],
         compiler_params=pltpu.CompilerParams(

time: 42.5 us -> 42.5 us (level)
  no operation moved by 1% of the time
where the time goes in v8:
time: 42.5 us; the launch traced here: 42.4 us
  Pallas kernels  42.4 us (100%)
    pallas_call x1, Pallas kernels, body(): pl.pallas_call(wide_kernel, name='wide', out_shape=(jax.ShapeDtypeStruct(...  38.6 us
    pallas_call x1, Pallas kernels, body(): pl.pallas_call(last_kernel, name='last', out_shape=jax.ShapeDtypeStruct((...  3.73 us

profile of v8, /device:TPU:1, one launch (start us, length us, event | category | flops | bytes accessed | tf_op | source)
XLA Modules:
  0.0 42.4 jit_solution(10407328685920708719)
XLA Ops:
  0.0 38.6 %wide.1 = (f32[32,8,128]{2,1,0:T(8,128)}, f32[32,32,256]{2,1,0:T(8,128)}) custom-call(f32[32,32,256]{2,1,0:T(8,128)} %bitcast.8, f32[64,16]{1,0:T(8,128)} %bitcast.9, f32[32,27]{1,0:T(8,128)} %depth_in.1, f32[32,32]{1,0:T(8,128)} %point_in.1, bf16[2,768,256]{2,1,0:T(8,128)(2,1)} %constant.12.clone.tx_in, f32[4,4,16,256]{3,2,1,0:T(8,128)} %constant.13.clone.ty_in, ...), custom_call_target="tpu_custom_call" | custom-call | tf_op jit(solution)/shard_map/wide/pallas_call | solution.py:551
  38.7 3.7 %last.1 = f32[32,32,256]{2,1,0:T(8,128)} custom-call(f32[32,8,128]{2,1,0:T(8,128)} %get-tuple-element.7.tiles_in, f32[32,32,256]{2,1,0:T(8,128)} %get-tuple-element.8.point_in, f32[4,4,32,128]{3,2,1,0:T(8,128)} %constant.14.clone.tyi_in, bf16[768,512]{1,0:T(8,128)(2,1)} %constant.17.clone.txi_in, f32[1,32]{1,0:T(1,128)} %bitcast.10), custom_call_target="tpu_custom_call" | custom-call | tf_op jit(solution)/shard_map/last/pallas_call | solution.py:599

commit v9 on v8

--- a/solution.py
+++ b/solution.py
@@ -169,13 +169,13 @@
     ]
     for load in loads[:3]:
         load.start()
+    for peer in plane_peers:
+        signal(plane_peer(peer)[0])
     for i in (2, ZC - 2, 1, ZC - 1):
         signal((ring_peer(i), gy))
     for dz in (-1, 1):
         for dy in (-1, 0, 1):
             signal(halo_peer(dz, dy))
-    for peer in plane_peers:
-        signal(plane_peer(peer)[0])
     loads[0].wait()
     for load in loads[3:]:
         load.start()

time: 42.5 us -> 42.6 us (level)
  no operation moved by 1% of the time
where the time goes in v9:
time: 42.6 us; the launch traced here: 42.4 us
  Pallas kernels  42.4 us (100%)
    pallas_call x1, Pallas kernels, body(): pl.pallas_call(wide_kernel, name='wide', out_shape=(jax.ShapeDtypeStruct(...  38.7 us
    pallas_call x1, Pallas kernels, body(): pl.pallas_call(last_kernel, name='last', out_shape=jax.ShapeDtypeStruct((...  3.74 us

profile of v9, /device:TPU:1, one launch (start us, length us, event | category | flops | bytes accessed | tf_op | source)
XLA Modules:
  0.0 42.4 jit_solution(4811644547522741322)
XLA Ops:
  0.0 38.7 %wide.1 = (f32[32,8,128]{2,1,0:T(8,128)}, f32[32,32,256]{2,1,0:T(8,128)}) custom-call(f32[32,32,256]{2,1,0:T(8,128)} %bitcast.8, f32[64,16]{1,0:T(8,128)} %bitcast.9, f32[32,27]{1,0:T(8,128)} %depth_in.1, f32[32,32]{1,0:T(8,128)} %point_in.1, bf16[2,768,256]{2,1,0:T(8,128)(2,1)} %constant.12.clone.tx_in, f32[4,4,16,256]{3,2,1,0:T(8,128)} %constant.13.clone.ty_in, ...), custom_call_target="tpu_custom_call" | custom-call | tf_op jit(solution)/shard_map/wide/pallas_call | solution.py:551
  38.7 3.7 %last.1 = f32[32,32,256]{2,1,0:T(8,128)} custom-call(f32[32,8,128]{2,1,0:T(8,128)} %get-tuple-element.7.tiles_in, f32[32,32,256]{2,1,0:T(8,128)} %get-tuple-element.8.point_in, f32[4,4,32,128]{3,2,1,0:T(8,128)} %constant.14.clone.tyi_in, bf16[768,512]{1,0:T(8,128)(2,1)} %constant.17.clone.txi_in, f32[1,32]{1,0:T(1,128)} %bitcast.10), custom_call_target="tpu_custom_call" | custom-call | tf_op jit(solution)/shard_map/last/pallas_call | solution.py:599
